TPU v7x, 256 devices: a whole 4x4x8 slice. The times are simulated.
256 devices in a mesh: post: 64 (over x, z, core), rep: 4 (over y).
Axes of the slice: x: 4, y: 4, z: 8, core: 2. Of those that a mesh axis runs over, the one named last changes fastest.
Arguments:
- split_vectors: bfloat16 [2048, 192, 1024], P('post', None, 'rep'), may hold values from -6 to 6
- split_labels: int32 [2048, 192], P('post'), may hold values from 0 to 1, as said below
- split_lengths: int32 [2048], P('post'), may hold values from 144 to 192
- new_owners: int32 [2048, 2], P('post'), may hold values from 0 to 63, all different within a row; in each aligned block of 32 rows (0 to 31, 32 to 63, ...) at most 2 rows name the same one
- neighbour_ids: int32 [2048, 64], replicated, may hold values from 0 to 511, all different within a row
- resident_vectors: bfloat16 [512, 192, 1024], P('post', None, 'rep'), may hold values from -6 to 6
- resident_centroids: bfloat16 [512, 1024], P('post', 'rep'), may hold values from -1 to 1
- resident_lengths: int32 [512], P('post'), may hold values from 1 to 192
Outputs:
- new_postings: bfloat16 [4096, 2, 96, 1024], P('post', None, None, 'rep')
- new_centroids: float32 [2048, 2, 1024], P('post', None, 'rep')
- rescore: float32 [512, 192], P('post')
Inputs may be any that keep to these rules, and one draw needn't show every extreme that they name: `split_labels`: rows at or past a posting's length carry label 1; each half of a split posting holds between 48 and 96 valid rows, and some split has both halves of exactly 96 rows. `new_owners`: the two halves of a split go to different owners; the halves of the splits of one index of post give at most 2 to any one owner. `neighbour_ids`: each split names 64 different postings.
All inputs are finite; a program needn't handle non-finite values.
Results may differ from a plain program's by a relative error of at most 0.0034.
Values may be sent and summed in bfloat16 or wider, within the bound.
No kernel may reach another device: no remote copies, remote signals or barrier semaphores. Data moves between devices by JAX's collectives and lax.ppermute only.
A program may use at most 128 MiB of HBM per device.

v0:
```python
import math

import jax
import jax.numpy as jnp
from jax import lax
from jax.sharding import PartitionSpec as P

D = 1024


far_value = 1e30


def nearest(best_dist, gathered, piece_start, row_data, row_norm, row_onehot, named_table):
    total_cents = gathered.shape[0]
    for block_start in range(0, total_cents, 512):
        block_width = min(512, total_cents - block_start)
        cent_block = gathered[block_start : block_start + block_width]
        cross = lax.dot_general(
            row_data, cent_block, (((1,), (1,)), ((), ())), preferred_element_type=jnp.float32
        )
        block_norm = jnp.einsum(
            "cd,cd->c", cent_block, cent_block, preferred_element_type=jnp.float32
        )
        distance = row_norm[:, None] - 2.0 * cross + block_norm[None, :]
        named_block = lax.dynamic_slice_in_dim(
            named_table, piece_start + block_start, block_width, 1
        )
        row_hits = jnp.dot(row_onehot, named_block, preferred_element_type=jnp.float32)
        distance = jnp.where(row_hits > 0.5, distance, far_value)
        best_dist = jnp.minimum(best_dist, jnp.min(distance, axis=1))
    return best_dist


def body(
    split_vectors,
    split_labels,
    split_lengths,
    new_owners,
    neighbour_ids,
    resident_vectors,
    resident_centroids,
    resident_lengths,
):
    n_post = lax.axis_size("post")
    s_local, length, dim_share = split_vectors.shape
    half_rows = length // 2
    hslot = max(2, 4 * s_local // n_post)
    row_ids = jnp.arange(length)
    is_valid = row_ids[None, :] < split_lengths[:, None]
    in_half = is_valid[:, None, :] & (split_labels[:, None, :] == jnp.arange(2)[None, :, None])
    member_int = in_half.astype(jnp.int32)
    half_rank = jnp.cumsum(member_int, axis=2) - member_int
    placement = in_half[:, :, None, :] & (
        half_rank[:, :, None, :] == jnp.arange(half_rows)[None, None, :, None]
    )
    packed = jnp.einsum(
        "shkr,srd->shkd",
        placement.astype(jnp.bfloat16),
        split_vectors,
        preferred_element_type=jnp.float32,
    ).astype(jnp.bfloat16)
    half_sums = jnp.einsum(
        "shr,srd->shd",
        in_half.astype(jnp.bfloat16),
        split_vectors,
        preferred_element_type=jnp.float32,
    )
    counts = jnp.sum(member_int, axis=2).astype(jnp.float32)
    new_centroids = half_sums / counts[:, :, None]
    owner_flat = new_owners.reshape(-1)
    half_order = jnp.arange(2 * s_local)
    same_owner = (owner_flat[:, None] == owner_flat[None, :]) & (
        half_order[None, :] < half_order[:, None]
    )
    slot_within = jnp.sum(same_owner.astype(jnp.int32), axis=1)
    target_slot = owner_flat * hslot + slot_within
    route_table = (jnp.arange(n_post * hslot)[:, None] == target_slot[None, :]).astype(jnp.bfloat16)
    outgoing = jnp.dot(
        route_table,
        packed.reshape(2 * s_local, half_rows * dim_share),
        preferred_element_type=jnp.float32,
    )
    outgoing = outgoing.astype(jnp.bfloat16).reshape(n_post, hslot, half_rows, dim_share)
    new_postings = lax.all_to_all(outgoing, "post", split_axis=0, concat_axis=0, tiled=True)
    res_local = resident_vectors.shape[0]
    own_diff = (
        resident_vectors.astype(jnp.float32) - resident_centroids.astype(jnp.float32)[:, None, :]
    )
    own_dist = lax.psum(jnp.sum(own_diff * own_diff, axis=2), "rep").reshape(-1)
    post_index = lax.axis_index("post")
    my_postings = post_index * res_local + jnp.arange(res_local)
    hits = jnp.any(neighbour_ids[:, :, None] == my_postings[None, None, :], axis=1)
    named_table = jnp.repeat(hits, 2, axis=0).T.astype(jnp.bfloat16)
    flat_rows = resident_vectors.reshape(res_local * length, dim_share)
    row_data = lax.all_gather(flat_rows, "rep", axis=1, tiled=True)
    row_posting = jnp.arange(res_local * length) // length
    row_norm = jnp.einsum("rd,rd->r", row_data, row_data, preferred_element_type=jnp.float32)
    row_onehot = (row_posting[:, None] == jnp.arange(res_local)[None, :]).astype(jnp.bfloat16)
    centroid_b = new_centroids.astype(jnp.bfloat16).reshape(2 * s_local, dim_share)
    all_shares = lax.all_gather(centroid_b, "post", axis=0, tiled=True)
    all_cents = lax.all_gather(all_shares, "rep", axis=1, tiled=True)
    best_dist = nearest(own_dist, all_cents, 0, row_data, row_norm, row_onehot, named_table)
    scores = (best_dist - row_norm) / math.sqrt(D)
    scores = scores.reshape(res_local, length)
    rescore = jnp.where(row_ids[None, :] < resident_lengths[:, None], scores, 0.0)
    return (new_postings, new_centroids, rescore)


def solution(mesh):
    return jax.shard_map(
        body,
        mesh=mesh,
        in_specs=(
            P("post", None, "rep"),
            P("post", None),
            P("post"),
            P("post", None),
            P(),
            P("post", None, "rep"),
            P("post", "rep"),
            P("post"),
        ),
        out_specs=(P("post", None, None, "rep"), P("post", None, "rep"), P("post", None)),
        check_vma=False,
    )
```

profile of v0, /device:TPU:1, one launch (start us, length us, event | category | flops | bytes accessed | tf_op | source)
XLA Modules:
  0.0 285.8 jit_solution(10616545221353187106)
XLA Ops:
  7.2 0.9 iota_compare_fusion.13
  8.1 0.9 convert_reduce_fusion
  9.0 0.1 copy.42
  9.1 1.2 fusion.101
  10.3 0.6 reshape.113
  11.0 0.7 all-gather.4.cloned.1.call-update
  11.8 1.2 reduce-window.6
  13.0 0.1 slice.44
  13.1 0.1 copy.37
  13.2 0.1 copy_bitcast_fusion
  13.4 1.6 fusion.39
  15.0 1.9 copy.83
  17.0 0.1 copy.34
  17.0 0.1 reshape.105
  17.1 0.2 convert_reduce_fusion.1
  17.3 75.5 %all-gather.6.cloned.1.call-done = bf16[4096,256]{1,0:T(8,128)(2,1)} async-done(((bf16[64,256]{1,0:T(8,128)(2,1)}), bf16[4096,256]{1,0:T(8,128)(2,1)}) %all-gather.6.cloned.1.call-update) | async-done | bytes 2097168 | tf_op jit(solution)/shard_map/all_gather | solution.py:101
  92.9 1.8 convolution_convert_fusion
  94.7 4.6 %copy.84 = bf16[16,8,96,256]{3,2,1,0:T(8,128)(2,1)} copy(bf16[16,8,96,256]{3,1,2,0:T(8,128)(2,1)S(1)} %bitcast.85) | data formatting | bytes 12582912
  99.3 7.0 %all-to-all-start = ((bf16[64,2,96,256]{3,2,1,0:T(8,128)(2,1)}), bf16[64,2,96,256]{3,2,1,0:T(8,128)(2,1)}, u32[]{:S(2)}, u32[]{:S(2)}) async-start(bf16[64,2,96,256]{3,2,1,0:T(8,128)(2,1)} %bitcast.84), calls=%async_computation | async-start | bytes 12582912 | tf_op jit(solution)/shard_map/all_to_all | solution.py:85
  106.3 0.7 compare_reduce_fusion
  107.0 0.4 copy.43
  107.4 1.0 broadcast_in_dim.15
  108.4 1.3 reshape.111
  109.8 0.4 multiply_reduce_fusion
  110.1 0.1 reshape.110
  110.2 9.5 %psum.7 = f32[1536]{0:T(1024)S(1)} all-reduce(f32[1536]{0:T(1024)S(1)} %reshape.110), channel_id=1, replica_groups=mesh['post'=64,'rep'=4] {'rep'}, use_global_device_ids=true, to_apply=%region_5.6 | all-reduce | flops 1536 | bytes 12288 | tf_op jit(solution)/shard_map/psum | solution.py:90
  119.7 2.4 fusion.75
  122.1 2.3 fusion.74
  124.4 2.3 fusion.73
  126.7 2.3 fusion.72
  129.0 2.4 fusion.71
  131.5 2.4 fusion.70
  133.9 2.4 fusion.69
  136.2 2.3 fusion.68
  138.5 2.7 fusion
  141.3 105.8 %all-to-all-done = bf16[64,2,96,256]{3,2,1,0:T(8,128)(2,1)} async-done(((bf16[64,2,96,256]{3,2,1,0:T(8,128)(2,1)}), bf16[64,2,96,256]{3,2,1,0:T(8,128)(2,1)}, u32[]{:S(2)}, u32[]{:S(2)}) %all-to-all-start) | async-done | bytes 6291488 | tf_op jit(solution)/shard_map/all_to_all | solution.py:85
  247.1 4.4 %fusion.51 = (f32[512]{0:T(512)S(1)}, f32[512]{0:T(512)S(1)}, f32[512]{0:T(512)S(1)}, f32[512]{0:T(512)S(1)}, f32[512]{0:T(512)S(1)}, /*index=5*/f32[512]{0:T(512)S(1)}, f32[512]{0:T(512)S(1)}, f32[512]{0:T(512)S(1)}) fusion(bf16[4096,1024]{1,0:T(8,128)(2,1)} %all-gather.8.cloned.1.call-done), kind=kLoop, calls=%fused_computation.66 | loop fusion | flops 12578816 | bytes 8404992 | tf_op jit(solution)/shard_map/cd,cd->c/dot_general | solution.py:22
  251.5 1.4 copy-done.2
  253.0 4.1 %fusion.52 = f32[1536]{0:T(1024)S(1)} fusion(f32[512]{0:T(512)S(1)} %get-tuple-element.3, bf16[1536,1024]{1,0:T(8,128)(2,1)S(1)} %copy-done.3, f32[1536]{0:T(1024)S(1)} %fusion, f32[1536,512]{0,1:T(8,128)} %fusion.75, bf16[4096,1024]{1,0:T(8,128)(2,1)S(1)} %copy-done.2), kind=kOutput, calls=%fused_computation.68 | convolution fusion | flops 1615329792 | bytes 7356416 | tf_op jit(solution)/shard_map/dot_general | solution.py:19
  257.1 2.1 fusion.53
  259.2 2.1 fusion.54
  261.3 2.1 fusion.55
  263.4 2.1 fusion.56
  265.6 2.1 fusion.57
  267.7 2.3 fusion.58
  270.0 2.1 fusion.59
  272.2 0.7 fusion.97
  272.9 6.5 %copy.93 = bf16[64,2,96,256]{3,2,1,0:T(8,128)(2,1)} copy(bf16[64,2,96,256]{3,2,1,0:T(8,128)(2,1)} %all-to-all-done) | data formatting | bytes 12582912
  (53 shorter events, 0.5 us)
Async XLA Ops:
  7.2 1.9 copy-start
  7.2 85.7 %all-gather.6.cloned.1.call-start = ((), (), s32[]{:S(2)}) async-start(), calls=%async_computation.2 | async-start | bytes 2129920 | tf_op jit(solution)/shard_map/all_gather | solution.py:101
  10.9 127.6 %all-gather.4.cloned.1.call-start = ((), (), s32[]{:S(2)}) async-start(), calls=%async_computation.1 | async-start | bytes 3932160 | tf_op jit(solution)/shard_map/all_gather | solution.py:96
  11.7 235.4 %all-gather.8.cloned.1.call-start = ((), (), s32[]{:S(2)}) async-start(), calls=%async_computation.3 | async-start | bytes 10485760 | tf_op jit(solution)/shard_map/all_gather | solution.py:102
  15.0 2.0 copy-start.14
  99.3 7.0 %copy-start.12 = (s32[2048,64]{0,1:T(8,128)S(1)}, s32[2048,64]{0,1:T(8,128)}, u32[]{:S(2)}) copy-start(s32[2048,64]{0,1:T(8,128)} %param.12) | copy-start | bytes 1572868
  99.3 147.8 %all-to-all-start = ((bf16[64,2,96,256]{3,2,1,0:T(8,128)(2,1)}), bf16[64,2,96,256]{3,2,1,0:T(8,128)(2,1)}, u32[]{:S(2)}, u32[]{:S(2)}) async-start(bf16[64,2,96,256]{3,2,1,0:T(8,128)(2,1)} %bitcast.84), calls=%async_computation | async-start | bytes 12582912 | tf_op jit(solution)/shard_map/all_to_all | solution.py:85
  106.2 3.5 %copy-start.13 = (bf16[8,256]{1,0:T(8,128)(2,1)S(1)}, bf16[8,256]{1,0:T(8,128)(2,1)}, u32[]{:S(2)}) copy-start(bf16[8,256]{1,0:T(8,128)(2,1)} %param.14) | copy-start | bytes 12292
  106.3 3.5 %copy-start.11 = (bf16[8,192,256]{2,1,0:T(8,128)(2,1)S(1)}, bf16[8,192,256]{2,1,0:T(8,128)(2,1)}, u32[]{:S(2)}) copy-start(bf16[8,192,256]{2,1,0:T(8,128)(2,1)} %param.13) | copy-start | bytes 2359300
  138.5 113.0 %copy-start.3 = (bf16[1536,1024]{1,0:T(8,128)(2,1)S(1)}, bf16[1536,1024]{1,0:T(8,128)(2,1)}, u32[]{:S(2)}) copy-start(bf16[1536,1024]{1,0:T(8,128)(2,1)} %all-gather.4.cloned.1.call-done) | copy-start | bytes 9437188
  247.1 5.9 %copy-start.2 = (bf16[4096,1024]{1,0:T(8,128)(2,1)S(1)}, bf16[4096,1024]{1,0:T(8,128)(2,1)}, u32[]{:S(2)}) copy-start(bf16[4096,1024]{1,0:T(8,128)(2,1)} %all-gather.8.cloned.1.call-done) | copy-start | bytes 25165828
  253.0 4.1 %copy-start.10 = (f32[1536,512]{0,1:T(8,128)S(1)}, f32[1536,512]{0,1:T(8,128)}, u32[]{:S(2)}) copy-start(f32[1536,512]{0,1:T(8,128)} %fusion.74) | copy-start | bytes 9437188
  257.1 2.1 copy-start.9
  259.2 2.1 copy-start.8
  261.3 2.1 copy-start.7
  263.4 2.1 copy-start.6
  265.5 2.1 copy-start.5
  267.7 2.3 copy-start.4
  270.0 2.2 copy-start.15
  272.9 6.5 %copy-start.1 = (bf16[32,192,256]{2,1,0:T(8,128)(2,1)S(1)}, bf16[32,192,256]{2,1,0:T(8,128)(2,1)}, u32[]{:S(2)}) copy-start(bf16[32,192,256]{2,1,0:T(8,128)(2,1)} %param.8) | copy-start | bytes 9437188
Sparse Core Ops, SparseCore 0:
  11.4 81.4 all-gather.5
  94.7 42.6 all-gather.3
  139.2 90.3 all-gather.7
where the time goes:
time: 286 us
  waiting for transfers between devices  182 us (64%)
  matrix products  42.2 us (15%)
  local copies, waits for them, and re-layouts  18.6 us (7%)
  between operations  14.2 us (5%)
  other arithmetic  12.2 us (4%)
  blocking collectives  9.52 us (3%)
  starting transfers between devices  7.1 us (2%)
    all_to_all x1, waiting for transfers between devices, body(): lax.all_to_all(outgoing, 'post', split_axis=0, concat_axis=0, tiled=True)  106 us
    all_gather x1, waiting for transfers between devices, body(): all_shares = lax.all_gather(centroid_b, 'post', axis=0, tiled=True)  75.5 us
    dot_general x8, matrix products, nearest(): lax.dot_general(row_data, cent_block, (((1,), (1,)), ((), ())), preferred...  18.9 us
    dot_general x8, matrix products, nearest(): jnp.dot(row_onehot, named_block, preferred_element_type=jnp.float32)  18.8 us
    unnamed x36, local copies, waits for them, and re-layouts  14.6 us
    psum x1, blocking collectives, body(): own_dist = lax.psum(jnp.sum(own_diff * own_diff, axis=2), 'rep').reshape(-1)  9.52 us
    all_to_all x1, starting transfers between devices, body(): lax.all_to_all(outgoing, 'post', split_axis=0, concat_axis=0, tiled=True)  6.98 us
  transfers between devices with their start and end apart: 4, of which 2 were waited for; matrix products, arithmetic and copies ran while one was open for 13% of the time, Pallas kernels for 0%

commit v1 on v0

v1 whole, which is shorter than its diff:
```python
import math

import jax
import jax.numpy as jnp
from jax import lax
from jax.experimental import pallas as pl
from jax.experimental.pallas import tpu as pltpu
from jax.sharding import PartitionSpec as P

D = 1024
far_value = 1e30


def pack_kernel(owners_hbm, lengths_hbm, labels_hbm, vectors_hbm, out_ref, cents_ref, cents_b_ref,
                owners_ref, lengths_ref, lengths_vec, labels_ref, vectors_ref, rank_ref, packed_ref,
                zero_ref, sums_ref, slot_ref, count_ref, out_sem, small_sem, in_sem):
    n_rep = cents_b_ref.shape[0]
    s_local, length = labels_ref.shape
    half_rows = length // 2
    n_owner = count_ref.shape[0]
    group = 4
    n_group = s_local // group

    def fetch(g):
        rows = pl.ds(g * group, group)
        return pltpu.make_async_copy(vectors_hbm.at[rows], vectors_ref.at[rows], in_sem.at[g])

    small = [
        pltpu.make_async_copy(owners_hbm, owners_ref, small_sem.at[0]),
        pltpu.make_async_copy(lengths_hbm, lengths_ref, small_sem.at[1]),
        pltpu.make_async_copy(lengths_hbm, lengths_vec.at[0], small_sem.at[2]),
        pltpu.make_async_copy(labels_hbm, labels_ref, small_sem.at[3]),
    ]
    for copy in small:
        copy.start()
    for g in range(n_group):
        fetch(g).start()
    zero_ref[...] = jnp.zeros_like(zero_ref)
    for o in range(n_owner):
        count_ref[o] = 0
    for copy in small:
        copy.wait()

    @pl.loop(0, s_local // 4)
    def _(g):
        for j in range(4):
            for h in range(2):
                s = g * 4 + j
                owner = owners_ref[h, s]
                slot_ref[2 * s + h] = owner * 2 + count_ref[owner]
                count_ref[owner] = count_ref[owner] + 1

    before = (
        lax.broadcasted_iota(jnp.int32, (length, length), 0)
        < lax.broadcasted_iota(jnp.int32, (length, length), 1)
    )
    labels = labels_ref[...].astype(jnp.float32)
    rank_ref[...] = jnp.dot(
        labels.astype(jnp.bfloat16),
        before.astype(jnp.float32).astype(jnp.bfloat16),
        preferred_element_type=jnp.float32,
    )
    row_id = lax.broadcasted_iota(jnp.int32, (1, length), 1)
    place_id = lax.broadcasted_iota(jnp.int32, (length, length), 0)
    sum_id = lax.broadcasted_iota(jnp.int32, (16, length), 0)

    @pl.loop(0, n_group)
    def _(g):
        fetch(g).wait()
        sums = []
        for j in range(group):
            s = g * group + j
            label = labels_ref[pl.ds(s, 1), :]
            rank = rank_ref[pl.ds(s, 1), :].astype(jnp.int32)
            half = jnp.where(row_id < lengths_ref[s], label, 2)
            goes_to = jnp.where(
                half == 0, row_id - rank, jnp.where(half == 1, half_rows + rank, length)
            )
            placement = jnp.concatenate(
                [
                    jnp.where(goes_to == place_id, 1.0, 0.0).astype(jnp.bfloat16),
                    jnp.where(half == sum_id, 1.0, 0.0).astype(jnp.bfloat16),
                ],
                axis=0,
            )
            placed = jnp.dot(placement, vectors_ref[s], preferred_element_type=jnp.float32)
            packed_ref[2 * s] = placed[:half_rows].astype(jnp.bfloat16)
            packed_ref[2 * s + 1] = placed[half_rows:length].astype(jnp.bfloat16)
            for h in range(2):
                pltpu.make_async_copy(
                    packed_ref.at[2 * s + h], out_ref.at[slot_ref[2 * s + h]], out_sem
                ).start()
            sums.append(placed[length : length + 2])
        sums_ref[pl.ds(pl.multiple_of(g * 8, 8), 8), :] = jnp.concatenate(sums, axis=0)

        for j in range(n_owner // n_group):
            o = g * (n_owner // n_group) + j
            for k in range(2):
                @pl.when(count_ref[o] <= k)
                def _():
                    pltpu.make_async_copy(zero_ref, out_ref.at[o * 2 + k], out_sem).start()

    ones_total = jnp.sum(labels, axis=1, keepdims=True)
    same = lax.broadcasted_iota(jnp.int32, (s_local, s_local), 0) == lax.broadcasted_iota(
        jnp.int32, (s_local, s_local), 1
    )
    lengths = jnp.sum(
        jnp.where(same, lengths_vec[...].astype(jnp.float32), 0.0), axis=1, keepdims=True
    )
    first = length - ones_total
    which = lax.broadcasted_iota(jnp.int32, (2 * s_local, s_local), 0)
    split_id = lax.broadcasted_iota(jnp.int32, (2 * s_local, s_local), 1)
    counts = 0.0
    for h, count in enumerate((first, lengths - first)):
        pick = jnp.where(which == 2 * split_id + h, 1.0, 0.0).astype(jnp.bfloat16)
        wide = jnp.broadcast_to(count, (s_local, 128)).astype(jnp.bfloat16)
        counts += jnp.dot(pick, wide, preferred_element_type=jnp.float32)
    cents = sums_ref[...] / jnp.concatenate([counts] * (sums_ref.shape[1] // 128), axis=1)
    cents_ref[...] = cents
    sums_ref[...] = cents
    share = 2 * s_local // n_rep
    rep = lax.axis_index("rep")
    for k in range(n_rep):
        start = pl.multiple_of(lax.rem(rep + k, n_rep) * share, share)
        cents_b_ref[k] = sums_ref[pl.ds(start, share), :].astype(jnp.bfloat16)
    pltpu.make_async_copy(out_ref, out_ref, out_sem).wait()


def pack(split_vectors, split_labels, split_lengths, new_owners, n_post, n_rep):
    s_local, length, dims = split_vectors.shape
    half_rows = length // 2
    return pl.pallas_call(
        pack_kernel,
        out_shape=(
            jax.ShapeDtypeStruct((2 * n_post, half_rows, dims), jnp.bfloat16),
            jax.ShapeDtypeStruct((2 * s_local, dims), jnp.float32),
            jax.ShapeDtypeStruct((n_rep, 2 * s_local // n_rep, dims), jnp.bfloat16),
        ),
        in_specs=[pl.BlockSpec(memory_space=pltpu.HBM)] * 4,
        out_specs=(
            pl.BlockSpec(memory_space=pltpu.HBM),
            pl.BlockSpec(memory_space=pltpu.VMEM),
            pl.BlockSpec(memory_space=pltpu.VMEM),
        ),
        scratch_shapes=[
            pltpu.SMEM((2, s_local), jnp.int32),
            pltpu.SMEM((s_local,), jnp.int32),
            pltpu.VMEM((1, s_local), jnp.int32),
            pltpu.VMEM((s_local, length), jnp.int32),
            pltpu.VMEM((s_local, length, dims), jnp.bfloat16),
            pltpu.VMEM((s_local, length), jnp.float32),
            pltpu.VMEM((2 * s_local, half_rows, dims), jnp.bfloat16),
            pltpu.VMEM((half_rows, dims), jnp.bfloat16),
            pltpu.VMEM((2 * s_local, dims), jnp.float32),
            pltpu.SMEM((2 * s_local,), jnp.int32),
            pltpu.SMEM((n_post,), jnp.int32),
            pltpu.SemaphoreType.DMA,
            pltpu.SemaphoreType.DMA((4,)),
            pltpu.SemaphoreType.DMA((s_local // 4,)),
        ],
        compiler_params=pltpu.CompilerParams(vmem_limit_bytes=56 << 20),
        cost_estimate=pl.CostEstimate(flops=10**9, bytes_accessed=16 << 20, transcendentals=0),
        name="pack",
    )(new_owners.T, split_lengths, split_labels, split_vectors)


def score_kernel(r0, r1, r2, r3, cents_ref, hits_ref, out_ref):
    rows = (r0, r1, r2, r3)
    n_q, length, dims = r0.shape
    blocks = [cents_ref[:, k].reshape(-1, dims) for k in range(len(rows))]
    norm = 0.0
    for block in blocks:
        wide = block.astype(jnp.float32)
        norm += jnp.sum(wide * wide, axis=1, keepdims=True)
    for q in range(n_q):
        cross = 0.0
        for block, ref in zip(blocks, rows):
            cross += lax.dot_general(
                block, ref[q], (((1,), (1,)), ((), ())), preferred_element_type=jnp.float32
            )
        offset = jnp.where(hits_ref[:, q : q + 1] > 0, norm, far_value)
        out_ref[q : q + 1, :] = jnp.min(offset - 2.0 * cross, axis=0, keepdims=True)


def score(rows, cents, hits):
    n_q, length, dims = rows[0].shape
    return pl.pallas_call(
        score_kernel,
        out_shape=jax.ShapeDtypeStruct((n_q, length), jnp.float32),
        in_specs=[pl.BlockSpec(memory_space=pltpu.VMEM)] * 6,
        out_specs=pl.BlockSpec(memory_space=pltpu.VMEM),
        compiler_params=pltpu.CompilerParams(vmem_limit_bytes=40 << 20),
        cost_estimate=pl.CostEstimate(flops=4 * 10**9, bytes_accessed=6 << 20, transcendentals=0),
        name="score",
    )(*rows, cents, hits)


def shift(x, axis, k):
    n = lax.axis_size(axis)
    return lax.ppermute(x, axis, [(i, (i + k) % n) for i in range(n)])


def body(
    split_vectors,
    split_labels,
    split_lengths,
    new_owners,
    neighbour_ids,
    resident_vectors,
    resident_centroids,
    resident_lengths,
):
    n_post, n_rep = lax.axis_size("post"), lax.axis_size("rep")
    s_local, length, dim_share = split_vectors.shape
    res_local = resident_vectors.shape[0]
    outgoing, new_centroids, centroid_b = pack(
        split_vectors, split_labels, split_lengths, new_owners, n_post, n_rep
    )
    new_centroids = new_centroids.reshape(s_local, 2, dim_share)
    outgoing = outgoing.reshape(n_post, 2, length // 2, dim_share)
    new_postings = lax.all_to_all(outgoing, "post", split_axis=0, concat_axis=0, tiled=True)

    rows = [resident_vectors] + [shift(resident_vectors, "rep", k) for k in range(1, n_rep)]
    my_cents = jnp.stack(
        [centroid_b[0]] + [shift(centroid_b[k], "rep", k) for k in range(1, n_rep)]
    )
    cents = lax.all_gather(
        my_cents.reshape(-1, n_rep * dim_share), "post", axis=0, tiled=True
    ).reshape(n_post, n_rep, -1, dim_share)
    my_ids = lax.dynamic_index_in_dim(
        neighbour_ids.reshape(n_post, n_rep, s_local // n_rep, -1),
        lax.axis_index("rep"), 1, keepdims=False,
    ).reshape(n_post * s_local // n_rep, -1)
    my_postings = lax.axis_index("post") * res_local + jnp.arange(res_local)
    hits = jnp.any(my_ids[:, :, None] == my_postings[None, None, :], axis=1)
    hits = jnp.repeat(hits.astype(jnp.int32), 2, axis=0)
    best = score(rows, cents, hits)

    wide_cents = resident_centroids.astype(jnp.float32)[:, None, :]
    own = jnp.sum(wide_cents * (wide_cents - 2.0 * resident_vectors.astype(jnp.float32)), axis=2)
    both = jnp.stack([best, own])
    one, two, three = (shift(both, "rep", k) for k in (1, 2, 3))
    best_all = jnp.minimum(jnp.minimum(best, two[0]), jnp.minimum(one[0], three[0]))
    own_all = (own + two[1]) + (one[1] + three[1])
    scores = jnp.minimum(best_all, own_all) / math.sqrt(D)
    row_ids = jnp.arange(length)
    rescore = jnp.where(row_ids[None, :] < resident_lengths[:, None], scores, 0.0)
    return (new_postings, new_centroids, rescore)


def solution(mesh):
    return jax.shard_map(
        body,
        mesh=mesh,
        in_specs=(
            P("post", None, "rep"),
            P("post", None),
            P("post"),
            P("post", None),
            P(),
            P("post", None, "rep"),
            P("post", "rep"),
            P("post"),
        ),
        out_specs=(P("post", None, None, "rep"), P("post", None, "rep"), P("post", None)),
        check_vma=False,
    )
```

time: 286 us -> 187 us (0.65)
  waiting for transfers between devices: 182 us -> 119 us
  matrix products: 42.2 us -> 0 us
  starting transfers between devices: 7.1 us -> 28.4 us
  Pallas kernels: 0 us -> 11.8 us
  other arithmetic: 12.2 us -> 1.27 us
  blocking collectives: 9.52 us -> 0 us
  local copies, waits for them, and re-layouts: 18.6 us -> 11.5 us
    all_to_all x1, waiting for transfers between devices: 106 us -> 27.1 us  [body(): lax.all_to_all(outgoing, 'post', split_axis=0, concat_axis=0, tiled=True)]
    dot_general x19 -> x0, matrix products: 42.2 us -> none  [the longest x8 18.9 us: nearest(): lax.dot_general(row_data, cent_block, (((1,), (1,)), ((), ())), preferred...]
    ppermute x0 -> x9, starting transfers between devices: none -> 15.1 us  [shift(): return lax.ppermute(x, axis, [(i, (i + k) % n) for i in range(n)])]
    all_gather x3 -> x1, waiting for transfers between devices: 75.5 us -> 89.1 us  [body(): lax.all_gather(my_cents.reshape(-1, n_rep * dim_share), 'post', axis=0, t...]
    pallas_call x0 -> x2, Pallas kernels: none -> 11.8 us  [the longest x1 6.25 us: score(): pl.pallas_call(score_kernel, out_shape=jax.ShapeDtypeStruct((n_q, length)...]
    psum x1 -> x0, blocking collectives: 9.52 us -> none  [body(): own_dist = lax.psum(jnp.sum(own_diff * own_diff, axis=2), 'rep').reshape(-1)]
    unnamed x36 -> x14, local copies, waits for them, and re-layouts: 14.6 us -> 6.66 us
    dot_general x2 -> x0, other arithmetic: 7.13 us -> none  [the longest x1 4.41 us: nearest(): jnp.einsum('cd,cd->c', cent_block, cent_block, preferred_element_type=jnp...]
  transfers between devices with their start and end apart: 4 -> 11, of which waited for: 2 -> 5; matrix products, arithmetic and copies ran while one was open for 13% -> 3% of each run, Pallas kernels for 0% -> 3%
where the time goes in v1:
time: 187 us; the launch traced here: 186 us
  waiting for transfers between devices  119 us (64%)
  starting transfers between devices  28.4 us (15%)
  between operations  14.3 us (8%)
  Pallas kernels  11.8 us (6%)
  local copies, waits for them, and re-layouts  11.5 us (6%)
    all_gather x1, waiting for transfers between devices, body(): lax.all_gather(my_cents.reshape(-1, n_rep * dim_share), 'post', axis=0, t...  89.1 us
    all_to_all x1, waiting for transfers between devices, body(): lax.all_to_all(outgoing, 'post', split_axis=0, concat_axis=0, tiled=True)  27.1 us
    ppermute x9, starting transfers between devices, shift(): return lax.ppermute(x, axis, [(i, (i + k) % n) for i in range(n)])  15.1 us
    all_to_all x1, starting transfers between devices, body(): lax.all_to_all(outgoing, 'post', split_axis=0, concat_axis=0, tiled=True)  13.3 us
    unnamed x14, local copies, waits for them, and re-layouts  6.66 us
    pallas_call x1, Pallas kernels, score(): pl.pallas_call(score_kernel, out_shape=jax.ShapeDtypeStruct((n_q, length)...  6.25 us
    pallas_call x1, Pallas kernels, pack(): pl.pallas_call(pack_kernel, out_shape=(jax.ShapeDtypeStruct((2 * n_post,...  5.57 us
  transfers between devices with their start and end apart: 11, of which 5 were waited for; matrix products, arithmetic and copies ran while one was open for 3% of the time, Pallas kernels for 3%

profile of v1, /device:TPU:1, one launch (start us, length us, event | category | flops | bytes accessed | tf_op | source)
XLA Modules:
  0.0 186.2 jit_solution(17762739314755607692)
XLA Ops:
  7.2 5.6 %pack.1 = (bf16[128,96,256]{2,1,0:T(8,128)(2,1)}, f32[64,256]{1,0:T(8,128)}, bf16[4,16,256]{2,1,0:T(8,128)(2,1)}) custom-call(s32[2,32]{1,0:T(2,128)} %bitcast.53, s32[32]{0:T(128)} %lengths_hbm.1, s32[32,192]{1,0:T(8,128)} %labels_hbm.1, bf16[32,192,256]{2,1,0:T(8,128)(2,1)} %vectors_hbm.1), custom_call_target="tpu_custom_call" | custom-call | flops 1000000000 | bytes 16777216 | tf_op jit(solution)/shard_map/pack/pallas_call | solution.py:132
  12.7 0.0 copy-start.3
  12.7 0.0 copy-start
  12.8 0.0 copy-start.1
  12.8 13.3 %all-to-all-start = ((bf16[64,2,96,256]{3,2,1,0:T(8,128)(2,1)}), bf16[64,2,96,256]{3,2,1,0:T(8,128)(2,1)}, u32[]{:S(2)}, u32[]{:S(2)}) async-start(bf16[64,2,96,256]{3,2,1,0:T(8,128)(2,1)} %bitcast.47), calls=%async_computation | async-start | bytes 12582912 | tf_op jit(solution)/shard_map/all_to_all | solution.py:221
  26.1 0.0 copy-start.4
  26.1 0.0 all-gather.2.cloned.1.call-start
  26.1 0.0 copy-done.3
  26.2 1.4 collective-permute-start.3
  27.5 2.6 %collective-permute-start.4 = (bf16[16,256]{1,0:T(8,128)(2,1)S(1)}, bf16[16,256]{1,0:T(8,128)(2,1)S(1)}, u32[]{:S(2)}, u32[]{:S(2)}) collective-permute-start(bf16[16,256]{1,0:T(8,128)(2,1)S(1)} %get-tuple-element.11), channel_id=1, source_target_pairs={{0,2},{1,3},{2,0},{3,1},{4,6},{5,7},{6,4},{7,5},{8,10},{9,11},{10,... | collective-permute-start | bytes 24584 | tf_op jit(solution)/shard_map/ppermute | solution.py:200
  30.2 1.1 collective-permute-start.5
  31.2 0.0 collective-permute-done.3
  31.2 0.3 collective-permute-done.4
  31.5 1.5 collective-permute-done.5
  33.1 0.6 reshape.36
  33.7 0.0 all-gather.2.cloned.1.call-update
  33.7 0.0 copy-done
  33.8 0.3 collective-permute-start
  34.0 3.3 %collective-permute-start.1 = (bf16[8,192,256]{2,1,0:T(8,128)(2,1)S(1)}, bf16[8,192,256]{2,1,0:T(8,128)(2,1)}, u32[]{:S(2)}, u32[]{:S(2)}) collective-permute-start(bf16[8,192,256]{2,1,0:T(8,128)(2,1)S(1)} %copy-done), channel_id=1, source_target_pairs={{0,2},{1,3},{2,0},{3,1},{4,6},{5,7},{6,4},{7,5},{8,10},{9,11},{10,... | collective-permute-start | bytes 2359304 | tf_op jit(solution)/shard_map/ppermute | solution.py:200
  37.3 0.1 collective-permute-start.2
  37.4 0.0 copy-done.1
  37.4 0.3 copy.12
  37.8 0.1 copy.13
  37.9 0.2 compare_reduce_fusion
  38.2 0.1 copy.14
  38.3 0.0 copy-done.4
  38.3 0.4 multiply_reduce_fusion
  38.7 89.1 %all-gather.2.cloned.1.call-done = bf16[1024,1024]{1,0:T(8,128)(2,1)} async-done(((bf16[16,1024]{1,0:T(8,128)(2,1)}), bf16[1024,1024]{1,0:T(8,128)(2,1)}) %all-gather.2.cloned.1.call-update) | async-done | bytes 2097168 | tf_op jit(solution)/shard_map/all_gather | solution.py:227
  127.8 3.1 %reshape.37.cents_ref = bf16[64,4,16,256]{3,2,1,0:T(8,128)(2,1)S(1)} reshape(bf16[1024,1024]{1,0:T(8,128)(2,1)} %all-gather.2.cloned.1.call-done) | data formatting | bytes 4194304 | tf_op jit(solution)/shard_map/reshape | solution.py:229
  130.9 0.0 collective-permute-done.r1
  130.9 0.0 collective-permute-done.1.r2
  130.9 0.0 collective-permute-done.2.r3
  130.9 0.2 broadcast_in_dim.5
  131.1 0.0 copy-start.2
  131.1 0.0 copy-start.5
  131.2 6.3 %score.1 = f32[8,192]{1,0:T(8,128)S(1)} custom-call(bf16[8,192,256]{2,1,0:T(8,128)(2,1)S(1)} %copy-done, bf16[8,192,256]{2,1,0:T(8,128)(2,1)} %collective-permute-done.r1, bf16[8,192,256]{2,1,0:T(8,128)(2,1)} %collective-permute-done.1.r2, bf16[8,192,256]{2,1,0:T(8,128)(2,1)} %collective-permute-done.2.r3, bf16[64,4,16,256]{3,2,1,0:T(8,128)(2,1)S(1)} %reshape.37.cents_ref, ...), custom_call_target="tpu_custom_call" | custom-call | flops 4000000000 | bytes 6291456 | tf_op jit(solution)/shard_map/score/pallas_call | solution.py:187
  137.4 3.7 %collective-permute-start.6 = (f32[2,8,192]{2,1,0:T(8,128)S(1)}, f32[2,8,192]{2,1,0:T(8,128)S(1)}, u32[]{:S(2)}, u32[]{:S(2)}) collective-permute-start(f32[2,8,192]{2,1,0:T(8,128)S(1)} %pad_maximum_fusion.1), channel_id=1, source_target_pairs={{0,2},{1,3},{2,0},{3,1},{4,6},{5,7},{6,4},{7,5},{8,10},{9,11},{10,... | collective-permute-start | bytes 36872 | tf_op jit(solution)/shard_map/ppermute | solution.py:200
  141.1 0.0 collective-permute-start.7
  141.1 2.7 %collective-permute-start.8 = (f32[2,8,192]{2,1,0:T(8,128)S(1)}, f32[2,8,192]{2,1,0:T(8,128)S(1)}, u32[]{:S(2)}, u32[]{:S(2)}) collective-permute-start(f32[2,8,192]{2,1,0:T(8,128)S(1)} %pad_maximum_fusion.1), channel_id=1, source_target_pairs={{0,3},{1,0},{2,1},{3,2},{4,7},{5,4},{6,5},{7,6},{8,11},{9,8},{10,9... | collective-permute-start | bytes 36872 | tf_op jit(solution)/shard_map/ppermute | solution.py:200
  143.8 0.0 copy-done.2
  143.8 0.7 reshape.35
  144.4 0.0 collective-permute-done.6
  144.4 0.8 collective-permute-done.7
  145.3 0.0 collective-permute-done.8
  145.3 0.0 copy-done.5
  145.3 0.7 fusion.4
  146.0 27.1 %all-to-all-done = bf16[64,2,96,256]{3,2,1,0:T(8,128)(2,1)} async-done(((bf16[64,2,96,256]{3,2,1,0:T(8,128)(2,1)}), bf16[64,2,96,256]{3,2,1,0:T(8,128)(2,1)}, u32[]{:S(2)}, u32[]{:S(2)}) %all-to-all-start) | async-done | bytes 6291488 | tf_op jit(solution)/shard_map/all_to_all | solution.py:221
  173.1 6.3 %copy.16 = bf16[64,2,96,256]{3,2,1,0:T(8,128)(2,1)} copy(bf16[64,2,96,256]{3,2,1,0:T(8,128)(2,1)} %all-to-all-done) | data formatting | bytes 12582912
  (7 shorter events, 0.1 us)
Async XLA Ops:
  12.7 13.4 %copy-start.3 = (bf16[4,16,256]{2,1,0:T(8,128)(2,1)S(1)}, bf16[4,16,256]{2,1,0:T(8,128)(2,1)}, u32[]{:S(2)}) copy-start(bf16[4,16,256]{2,1,0:T(8,128)(2,1)} %get-tuple-element.8) | copy-start | bytes 98308
  12.7 21.0 %copy-start = (bf16[8,192,256]{2,1,0:T(8,128)(2,1)S(1)}, bf16[8,192,256]{2,1,0:T(8,128)(2,1)}, u32[]{:S(2)}) copy-start(bf16[8,192,256]{2,1,0:T(8,128)(2,1)} %r0.1) | copy-start | bytes 2359300
  12.8 24.7 %copy-start.1 = (s32[2048,64]{0,1:T(8,128)S(1)}, s32[2048,64]{0,1:T(8,128)}, u32[]{:S(2)}) copy-start(s32[2048,64]{0,1:T(8,128)} %param.12) | copy-start | bytes 1572868
  12.8 160.3 %all-to-all-start = ((bf16[64,2,96,256]{3,2,1,0:T(8,128)(2,1)}), bf16[64,2,96,256]{3,2,1,0:T(8,128)(2,1)}, u32[]{:S(2)}, u32[]{:S(2)}) async-start(bf16[64,2,96,256]{3,2,1,0:T(8,128)(2,1)} %bitcast.47), calls=%async_computation | async-start | bytes 12582912 | tf_op jit(solution)/shard_map/all_to_all | solution.py:221
  26.1 12.2 %copy-start.4 = (bf16[8,256]{1,0:T(8,128)(2,1)S(1)}, bf16[8,256]{1,0:T(8,128)(2,1)}, u32[]{:S(2)}) copy-start(bf16[8,256]{1,0:T(8,128)(2,1)} %param.14) | copy-start | bytes 12292
  26.1 101.7 %all-gather.2.cloned.1.call-start = ((), (), s32[]{:S(2)}) async-start(), calls=%async_computation.1 | async-start | bytes 2129920 | tf_op jit(solution)/shard_map/all_gather | solution.py:227
  26.2 5.1 %collective-permute-start.3 = (bf16[16,256]{1,0:T(8,128)(2,1)S(1)}, bf16[16,256]{1,0:T(8,128)(2,1)S(1)}, u32[]{:S(2)}, u32[]{:S(2)}) collective-permute-start(bf16[16,256]{1,0:T(8,128)(2,1)S(1)} %get-tuple-element.12), channel_id=1, source_target_pairs={{0,1},{1,2},{2,3},{3,0},{4,5},{5,6},{6,7},{7,4},{8,9},{9,10},{10,1... | collective-permute-start | bytes 24584 | tf_op jit(solution)/shard_map/ppermute | solution.py:200
  27.5 4.0 %collective-permute-start.4 = (bf16[16,256]{1,0:T(8,128)(2,1)S(1)}, bf16[16,256]{1,0:T(8,128)(2,1)S(1)}, u32[]{:S(2)}, u32[]{:S(2)}) collective-permute-start(bf16[16,256]{1,0:T(8,128)(2,1)S(1)} %get-tuple-element.11), channel_id=1, source_target_pairs={{0,2},{1,3},{2,0},{3,1},{4,6},{5,7},{6,4},{7,5},{8,10},{9,11},{10,... | collective-permute-start | bytes 24584 | tf_op jit(solution)/shard_map/ppermute | solution.py:200
  30.2 2.9 %collective-permute-start.5 = (bf16[16,256]{1,0:T(8,128)(2,1)S(1)}, bf16[16,256]{1,0:T(8,128)(2,1)S(1)}, u32[]{:S(2)}, u32[]{:S(2)}) collective-permute-start(bf16[16,256]{1,0:T(8,128)(2,1)S(1)} %get-tuple-element.10), channel_id=1, source_target_pairs={{0,3},{1,0},{2,1},{3,2},{4,7},{5,4},{6,5},{7,6},{8,11},{9,8},{10,9... | collective-permute-start | bytes 24584 | tf_op jit(solution)/shard_map/ppermute | solution.py:200
  33.8 97.2 %collective-permute-start = (bf16[8,192,256]{2,1,0:T(8,128)(2,1)S(1)}, bf16[8,192,256]{2,1,0:T(8,128)(2,1)}, u32[]{:S(2)}, u32[]{:S(2)}) collective-permute-start(bf16[8,192,256]{2,1,0:T(8,128)(2,1)S(1)} %copy-done), channel_id=1, source_target_pairs={{0,1},{1,2},{2,3},{3,0},{4,5},{5,6},{6,7},{7,4},{8,9},{9,10},{10,1... | collective-permute-start | bytes 2359304 | tf_op jit(solution)/shard_map/ppermute | solution.py:200
  34.0 96.9 %collective-permute-start.1 = (bf16[8,192,256]{2,1,0:T(8,128)(2,1)S(1)}, bf16[8,192,256]{2,1,0:T(8,128)(2,1)}, u32[]{:S(2)}, u32[]{:S(2)}) collective-permute-start(bf16[8,192,256]{2,1,0:T(8,128)(2,1)S(1)} %copy-done), channel_id=1, source_target_pairs={{0,2},{1,3},{2,0},{3,1},{4,6},{5,7},{6,4},{7,5},{8,10},{9,11},{10,... | collective-permute-start | bytes 2359304 | tf_op jit(solution)/shard_map/ppermute | solution.py:200
  37.3 93.6 %collective-permute-start.2 = (bf16[8,192,256]{2,1,0:T(8,128)(2,1)S(1)}, bf16[8,192,256]{2,1,0:T(8,128)(2,1)}, u32[]{:S(2)}, u32[]{:S(2)}) collective-permute-start(bf16[8,192,256]{2,1,0:T(8,128)(2,1)S(1)} %copy-done), channel_id=1, source_target_pairs={{0,3},{1,0},{2,1},{3,2},{4,7},{5,4},{6,5},{7,6},{8,11},{9,8},{10,9... | collective-permute-start | bytes 2359304 | tf_op jit(solution)/shard_map/ppermute | solution.py:200
  131.1 12.6 %copy-start.2 = (f32[64,256]{1,0:T(8,128)S(1)}, f32[64,256]{1,0:T(8,128)}, u32[]{:S(2)}) copy-start(f32[64,256]{1,0:T(8,128)} %get-tuple-element.7) | copy-start | bytes 196612
  131.1 14.2 %copy-start.5 = (s32[8]{0:T(128)S(1)}, s32[8]{0:T(128)}, u32[]{:S(2)}) copy-start(s32[8]{0:T(128)} %param.15) | copy-start | bytes 100
  137.4 7.0 %collective-permute-start.6 = (f32[2,8,192]{2,1,0:T(8,128)S(1)}, f32[2,8,192]{2,1,0:T(8,128)S(1)}, u32[]{:S(2)}, u32[]{:S(2)}) collective-permute-start(f32[2,8,192]{2,1,0:T(8,128)S(1)} %pad_maximum_fusion.1), channel_id=1, source_target_pairs={{0,2},{1,3},{2,0},{3,1},{4,6},{5,7},{6,4},{7,5},{8,10},{9,11},{10,... | collective-permute-start | bytes 36872 | tf_op jit(solution)/shard_map/ppermute | solution.py:200
  141.1 4.2 %collective-permute-start.7 = (f32[2,8,192]{2,1,0:T(8,128)S(1)}, f32[2,8,192]{2,1,0:T(8,128)S(1)}, u32[]{:S(2)}, u32[]{:S(2)}) collective-permute-start(f32[2,8,192]{2,1,0:T(8,128)S(1)} %pad_maximum_fusion.1), channel_id=1, source_target_pairs={{0,1},{1,2},{2,3},{3,0},{4,5},{5,6},{6,7},{7,4},{8,9},{9,10},{10,1... | collective-permute-start | bytes 36872 | tf_op jit(solution)/shard_map/ppermute | solution.py:200
  141.1 4.2 %collective-permute-start.8 = (f32[2,8,192]{2,1,0:T(8,128)S(1)}, f32[2,8,192]{2,1,0:T(8,128)S(1)}, u32[]{:S(2)}, u32[]{:S(2)}) collective-permute-start(f32[2,8,192]{2,1,0:T(8,128)S(1)} %pad_maximum_fusion.1), channel_id=1, source_target_pairs={{0,3},{1,0},{2,1},{3,2},{4,7},{5,4},{6,5},{7,6},{8,11},{9,8},{10,9... | collective-permute-start | bytes 36872 | tf_op jit(solution)/shard_map/ppermute | solution.py:200
Sparse Core Ops, SparseCore 0:
  33.9 93.8 all-gather.1

commit v2 on v1

v2 whole, which is shorter than its diff:
```python
import functools
import math

import jax
import jax.numpy as jnp
from jax import lax
from jax.experimental import pallas as pl
from jax.experimental.pallas import tpu as pltpu
from jax.sharding import PartitionSpec as P

D = 1024
far_value = 1e30
N_X, N_Z, N_CORE = 4, 8, 2


def centroid_kernel(lengths_hbm, labels_hbm, vectors_hbm, cents_ref, copies_ref,
                    lengths_vec, labels_ref, vectors_ref, sums_ref, half_ref, small_sem, in_sem):
    s_local, length = labels_ref.shape
    group = 4
    n_group = s_local // group

    def fetch(g):
        rows = pl.ds(g * group, group)
        return pltpu.make_async_copy(vectors_hbm.at[rows], vectors_ref.at[rows], in_sem.at[g])

    small = [
        pltpu.make_async_copy(lengths_hbm, lengths_vec.at[0], small_sem.at[0]),
        pltpu.make_async_copy(labels_hbm, labels_ref, small_sem.at[1]),
    ]
    for copy in small:
        copy.start()
    for g in range(n_group):
        fetch(g).start()
    for copy in small:
        copy.wait()

    same = lax.broadcasted_iota(jnp.int32, (s_local, s_local), 0) == lax.broadcasted_iota(
        jnp.int32, (s_local, s_local), 1
    )
    lengths = jnp.sum(
        jnp.where(same, lengths_vec[...].astype(jnp.float32), 0.0), axis=1, keepdims=True
    )
    row_id = lax.broadcasted_iota(jnp.int32, (s_local, length), 1).astype(jnp.float32)
    half_ref[...] = jnp.where(row_id < lengths, labels_ref[...], 2)
    sum_id = lax.broadcasted_iota(jnp.int32, (16, length), 0)
    for g in range(n_group):
        fetch(g).wait()
        sums = []
        for s in range(g * group, (g + 1) * group):
            member = jnp.where(half_ref[s : s + 1, :] == sum_id, 1.0, 0.0).astype(jnp.bfloat16)
            sums.append(
                jnp.dot(member, vectors_ref[s], preferred_element_type=jnp.float32)[:2]
            )
        sums_ref[g * 8 : g * 8 + 8, :] = jnp.concatenate(sums, axis=0)

    which = lax.broadcasted_iota(jnp.int32, (2 * s_local, s_local), 0)
    split_id = lax.broadcasted_iota(jnp.int32, (2 * s_local, s_local), 1)
    counts = 0.0
    for h in range(2):
        count = jnp.sum(jnp.where(half_ref[...] == h, 1.0, 0.0), axis=1, keepdims=True)
        pick = jnp.where(which == 2 * split_id + h, 1.0, 0.0).astype(jnp.bfloat16)
        wide = jnp.broadcast_to(count, (s_local, 128)).astype(jnp.bfloat16)
        counts += jnp.dot(pick, wide, preferred_element_type=jnp.float32)
    cents = sums_ref[...] / jnp.concatenate([counts] * (sums_ref.shape[1] // 128), axis=1)
    cents_ref[...] = cents
    rounded = cents.astype(jnp.bfloat16)
    for i in range(copies_ref.shape[0]):
        copies_ref[i] = rounded


def centroids(split_vectors, split_labels, split_lengths):
    s_local, length, dims = split_vectors.shape
    return pl.pallas_call(
        centroid_kernel,
        out_shape=(
            jax.ShapeDtypeStruct((2 * s_local, dims), jnp.float32),
            jax.ShapeDtypeStruct((N_Z, 2 * s_local, dims), jnp.bfloat16),
        ),
        in_specs=[pl.BlockSpec(memory_space=pltpu.HBM)] * 3,
        out_specs=(pl.BlockSpec(memory_space=pltpu.VMEM),) * 2,
        scratch_shapes=[
            pltpu.VMEM((1, s_local), jnp.int32),
            pltpu.VMEM((s_local, length), jnp.int32),
            pltpu.VMEM((s_local, length, dims), jnp.bfloat16),
            pltpu.VMEM((2 * s_local, dims), jnp.float32),
            pltpu.VMEM((s_local, length), jnp.int32),
            pltpu.SemaphoreType.DMA((2,)),
            pltpu.SemaphoreType.DMA((s_local // 4,)),
        ],
        compiler_params=pltpu.CompilerParams(vmem_limit_bytes=56 << 20),
        cost_estimate=pl.CostEstimate(flops=10**8, bytes_accessed=4 << 20, transcendentals=0),
        name="centroids",
    )(split_lengths, split_labels, split_vectors)


def pack_kernel(owners_hbm, lengths_hbm, labels_hbm, vectors_hbm, out_ref,
                owners_ref, lengths_ref, labels_ref, vectors_ref, rank_ref, packed_ref,
                zero_ref, slot_ref, count_ref, out_sem, small_sem, in_sem):
    s_local, length = labels_ref.shape
    half_rows = length // 2
    n_owner = count_ref.shape[0]
    group = 4
    n_group = s_local // group

    def fetch(g):
        rows = pl.ds(g * group, group)
        return pltpu.make_async_copy(vectors_hbm.at[rows], vectors_ref.at[rows], in_sem.at[g])

    small = [
        pltpu.make_async_copy(owners_hbm, owners_ref, small_sem.at[0]),
        pltpu.make_async_copy(lengths_hbm, lengths_ref, small_sem.at[1]),
        pltpu.make_async_copy(labels_hbm, labels_ref, small_sem.at[2]),
    ]
    for copy in small:
        copy.start()
    for g in range(n_group):
        fetch(g).start()
    zero_ref[...] = jnp.zeros_like(zero_ref)
    for o in range(n_owner):
        count_ref[o] = 0
    for copy in small:
        copy.wait()

    @pl.loop(0, s_local // 4)
    def _(g):
        for j in range(4):
            for h in range(2):
                s = g * 4 + j
                owner = owners_ref[h, s]
                slot_ref[2 * s + h] = owner * 2 + count_ref[owner]
                count_ref[owner] = count_ref[owner] + 1

    before = (
        lax.broadcasted_iota(jnp.int32, (length, length), 0)
        < lax.broadcasted_iota(jnp.int32, (length, length), 1)
    )
    labels = labels_ref[...].astype(jnp.float32)
    rank_ref[...] = jnp.dot(
        labels.astype(jnp.bfloat16),
        before.astype(jnp.float32).astype(jnp.bfloat16),
        preferred_element_type=jnp.float32,
    )
    row_id = lax.broadcasted_iota(jnp.int32, (1, length), 1)
    place_id = lax.broadcasted_iota(jnp.int32, (length, length), 0)

    @pl.loop(0, n_group)
    def _(g):
        fetch(g).wait()
        for j in range(group):
            s = g * group + j
            label = labels_ref[pl.ds(s, 1), :]
            rank = rank_ref[pl.ds(s, 1), :].astype(jnp.int32)
            half = jnp.where(row_id < lengths_ref[s], label, 2)
            goes_to = jnp.where(
                half == 0, row_id - rank, jnp.where(half == 1, half_rows + rank, length)
            )
            placement = jnp.where(goes_to == place_id, 1.0, 0.0).astype(jnp.bfloat16)
            placed = jnp.dot(placement, vectors_ref[s], preferred_element_type=jnp.float32)
            packed_ref[2 * s] = placed[:half_rows].astype(jnp.bfloat16)
            packed_ref[2 * s + 1] = placed[half_rows:length].astype(jnp.bfloat16)
            for h in range(2):
                pltpu.make_async_copy(
                    packed_ref.at[2 * s + h], out_ref.at[slot_ref[2 * s + h]], out_sem
                ).start()

        for j in range(n_owner // n_group):
            o = g * (n_owner // n_group) + j
            for k in range(2):
                @pl.when(count_ref[o] <= k)
                def _():
                    pltpu.make_async_copy(zero_ref, out_ref.at[o * 2 + k], out_sem).start()

    pltpu.make_async_copy(out_ref, out_ref, out_sem).wait()


def pack(split_vectors, split_labels, split_lengths, new_owners, n_post):
    s_local, length, dims = split_vectors.shape
    half_rows = length // 2
    return pl.pallas_call(
        pack_kernel,
        out_shape=jax.ShapeDtypeStruct((2 * n_post, half_rows, dims), jnp.bfloat16),
        in_specs=[pl.BlockSpec(memory_space=pltpu.HBM)] * 4,
        out_specs=pl.BlockSpec(memory_space=pltpu.HBM),
        scratch_shapes=[
            pltpu.SMEM((2, s_local), jnp.int32),
            pltpu.SMEM((s_local,), jnp.int32),
            pltpu.VMEM((s_local, length), jnp.int32),
            pltpu.VMEM((s_local, length, dims), jnp.bfloat16),
            pltpu.VMEM((s_local, length), jnp.float32),
            pltpu.VMEM((2 * s_local, half_rows, dims), jnp.bfloat16),
            pltpu.VMEM((half_rows, dims), jnp.bfloat16),
            pltpu.SMEM((2 * s_local,), jnp.int32),
            pltpu.SMEM((n_post,), jnp.int32),
            pltpu.SemaphoreType.DMA,
            pltpu.SemaphoreType.DMA((3,)),
            pltpu.SemaphoreType.DMA((s_local // 4,)),
        ],
        compiler_params=pltpu.CompilerParams(vmem_limit_bytes=56 << 20),
        cost_estimate=pl.CostEstimate(flops=10**9, bytes_accessed=16 << 20, transcendentals=0),
        name="pack",
    )(new_owners.T, split_lengths, split_labels, split_vectors)


def score_kernel(*refs):
    n_rows = len(refs) - N_X * N_CORE - 2
    rows, pieces = refs[:n_rows], refs[n_rows:-2]
    hits_ref, out_ref = refs[-2:]
    n_q = rows[0].shape[0]
    blocks = [jnp.concatenate([p[k] for p in pieces], axis=0) for k in range(n_rows)]
    norm = 0.0
    for block in blocks:
        wide = block.astype(jnp.float32)
        norm += jnp.sum(wide * wide, axis=1, keepdims=True)
    for q in range(n_q):
        cross = 0.0
        for block, ref in zip(blocks, rows):
            cross += lax.dot_general(
                block, ref[q], (((1,), (1,)), ((), ())), preferred_element_type=jnp.float32
            )
        offset = jnp.where(hits_ref[:, q : q + 1] > 0, norm, far_value)
        out_ref[q : q + 1, :] = jnp.min(offset - 2.0 * cross, axis=0, keepdims=True)


def score(rows, pieces, hits):
    n_q, length, dims = rows[0].shape
    return pl.pallas_call(
        score_kernel,
        out_shape=jax.ShapeDtypeStruct((n_q, length), jnp.float32),
        in_specs=[pl.BlockSpec(memory_space=pltpu.VMEM)] * (len(rows) + len(pieces) + 1),
        out_specs=pl.BlockSpec(memory_space=pltpu.VMEM),
        compiler_params=pltpu.CompilerParams(vmem_limit_bytes=40 << 20),
        cost_estimate=pl.CostEstimate(flops=4 * 10**9, bytes_accessed=6 << 20, transcendentals=0),
        name="score",
    )(*rows, *pieces, hits)


def store_kernel(got, out, held, in_sems, out_sems):
    n_copies = in_sems.shape[0]
    step = got.shape[0] // n_copies
    rows = [pl.ds(i * step, step) for i in range(n_copies)]
    reads = [
        pltpu.make_async_copy(got.at[r], held.at[r], in_sems.at[i]) for i, r in enumerate(rows)
    ]
    writes = [
        pltpu.make_async_copy(held.at[r], out.at[r], out_sems.at[i]) for i, r in enumerate(rows)
    ]
    for read in reads:
        read.start()
    for read, write in zip(reads, writes):
        read.wait()
        write.start()
    for write in writes:
        write.wait()


def store(got):
    n_copies = 16
    return pl.pallas_call(
        store_kernel,
        out_shape=jax.ShapeDtypeStruct(got.shape, got.dtype),
        in_specs=[pl.BlockSpec(memory_space=pltpu.HBM)],
        out_specs=pl.BlockSpec(memory_space=pltpu.HBM),
        scratch_shapes=[
            pltpu.VMEM(got.shape, got.dtype),
            pltpu.SemaphoreType.DMA((n_copies,)),
            pltpu.SemaphoreType.DMA((n_copies,)),
        ],
        compiler_params=pltpu.CompilerParams(vmem_limit_bytes=56 << 20),
        cost_estimate=pl.CostEstimate(flops=0, bytes_accessed=12 << 20, transcendentals=0),
        name="store",
    )(got)


def shift(x, axis, k):
    n = lax.axis_size(axis)
    return lax.ppermute(x, axis, [(i, (i + k) % n) for i in range(n)])


def shift_in_plane(x, by_x, by_core):
    pairs = []
    for i in range(N_X * N_Z * N_CORE):
        at_x, at_z, core = i // (N_Z * N_CORE), i // N_CORE % N_Z, i % N_CORE
        to = ((at_x + by_x) % N_X * N_Z + at_z) * N_CORE + (core + by_core) % N_CORE
        pairs.append((i, to))
    return lax.ppermute(x, "post", pairs)


def body(
    split_vectors,
    split_labels,
    split_lengths,
    new_owners,
    neighbour_ids,
    resident_vectors,
    resident_centroids,
    resident_lengths,
):
    n_post, n_rep = lax.axis_size("post"), lax.axis_size("rep")
    s_local, length, dim_share = split_vectors.shape
    res_local = resident_vectors.shape[0]
    new_centroids, copies = centroids(split_vectors, split_labels, split_lengths)

    z_groups = [
        [(x * N_Z + z) * N_CORE + core for z in range(N_Z)]
        for x in range(N_X) for core in range(N_CORE)
    ]
    on_z = lax.all_to_all(
        copies, "post", split_axis=0, concat_axis=0, tiled=True, axis_index_groups=z_groups
    )
    new_centroids, split_vectors = lax.optimization_barrier((new_centroids, split_vectors))
    outgoing = pack(split_vectors, split_labels, split_lengths, new_owners, n_post)
    on_z, outgoing, resident_vectors, resident_centroids, neighbour_ids = lax.optimization_barrier(
        (on_z, outgoing, resident_vectors, resident_centroids, neighbour_ids)
    )
    outgoing = outgoing.reshape(n_post, 2, length // 2, dim_share)
    new_postings = store(
        lax.all_to_all(outgoing, "post", split_axis=0, concat_axis=0, tiled=True)
    )
    new_centroids = new_centroids.reshape(s_local, 2, dim_share)

    rep, post = lax.axis_index("rep"), lax.axis_index("post")
    per_rep = N_Z // n_rep
    parts = [
        lax.dynamic_slice_in_dim(on_z, lax.rem(rep + k, n_rep) * per_rep, per_rep).reshape(
            per_rep * 2 * s_local, dim_share
        )
        for k in range(n_rep)
    ]
    mine = jnp.stack([parts[0]] + [shift(parts[k], "rep", k) for k in range(1, n_rep)])
    pieces = [mine] + [shift_in_plane(mine, k, 0) for k in (1, 3, 2)]
    pieces += [shift_in_plane(piece, 0, 1) for piece in pieces]
    rows = [resident_vectors] + [shift(resident_vectors, "rep", k) for k in range(1, n_rep)]

    my_postings = post * res_local + jnp.arange(res_local)
    ids = []
    for by_core in (0, 1):
        for by_x in (0, 1, 3, 2):
            from_x = lax.rem(post // (N_Z * N_CORE) + N_X - by_x, N_X)
            from_core = lax.rem(post + by_core, N_CORE)
            for z in range(per_rep):
                source = (from_x * N_Z + rep * per_rep + z) * N_CORE + from_core
                ids.append(lax.dynamic_slice_in_dim(neighbour_ids, source * s_local, s_local))
    hits = jnp.any(jnp.concatenate(ids)[:, :, None] == my_postings[None, None, :], axis=1)
    hits = jnp.repeat(hits.astype(jnp.int32), 2, axis=0)
    wide_cents = resident_centroids.astype(jnp.float32)[:, None, :]
    own = jnp.sum(wide_cents * (wide_cents - 2.0 * resident_vectors.astype(jnp.float32)), axis=2)
    best = score(rows, pieces, hits)
    both = jnp.stack([best, own])
    one, two, three = (shift(both, "rep", k) for k in (1, 2, 3))
    best_all = jnp.minimum(jnp.minimum(best, two[0]), jnp.minimum(one[0], three[0]))
    own_all = (own + two[1]) + (one[1] + three[1])
    scores = jnp.minimum(best_all, own_all) / math.sqrt(D)
    row_ids = jnp.arange(length)
    rescore = jnp.where(row_ids[None, :] < resident_lengths[:, None], scores, 0.0)
    return (new_postings, new_centroids, rescore)


def solution(mesh):
    return jax.shard_map(
        body,
        mesh=mesh,
        in_specs=(
            P("post", None, "rep"),
            P("post", None),
            P("post"),
            P("post", None),
            P(),
            P("post", None, "rep"),
            P("post", "rep"),
            P("post"),
        ),
        out_specs=(P("post", None, None, "rep"), P("post", None, "rep"), P("post", None)),
        check_vma=False,
    )
```

time: 187 us -> 179 us (0.957)
  between operations: 14.3 us -> 1 us
  starting transfers between devices: 28.4 us -> 40 us
  waiting for transfers between devices: 119 us -> 109 us
  Pallas kernels: 11.8 us -> 20.2 us
  local copies, waits for them, and re-layouts: 11.5 us -> 7.12 us
    all_gather x1 -> x0, waiting for transfers between devices: 89.1 us -> none  [body(): lax.all_gather(my_cents.reshape(-1, n_rep * dim_share), 'post', axis=0, t...]
    all_to_all x1, waiting for transfers between devices: 27.1 us -> 76.8 us  [body(): lax.all_to_all(outgoing, 'post', split_axis=0, concat_axis=0, tiled=True)]
    ppermute x0 -> x7, waiting for transfers between devices: none -> 16.7 us  [shift_in_plane(): return lax.ppermute(x, 'post', pairs)]
    all_to_all x0 -> x1, starting transfers between devices: none -> 9.03 us  [body(): lax.all_to_all(copies, 'post', split_axis=0, concat_axis=0, tiled=True, a...]
    pallas_call x1 -> x3, Pallas kernels: 5.57 us -> 14.3 us  [the longest x1 5.48 us: store(): pl.pallas_call(store_kernel, out_shape=jax.ShapeDtypeStruct(got.shape, go...]
    ppermute x0 -> x7, starting transfers between devices: none -> 6.94 us  [shift_in_plane(): return lax.ppermute(x, 'post', pairs)]
    ppermute x9, waiting for transfers between devices: 2.69 us -> 9.62 us  [shift(): return lax.ppermute(x, axis, [(i, (i + k) % n) for i in range(n)])]
    unnamed x14 -> x16, local copies, waits for them, and re-layouts: 6.66 us -> 0.73 us
  transfers between devices with their start and end apart: 11 -> 18, of which waited for: 5 -> 11; matrix products, arithmetic and copies ran while one was open for 3% -> 4% of each run, Pallas kernels for 3% -> 6%
where the time goes in v2:
time: 179 us; the launch traced here: 178 us
  waiting for transfers between devices  109 us (61%)
  starting transfers between devices  40 us (22%)
  Pallas kernels  20.2 us (11%)
  local copies, waits for them, and re-layouts  7.12 us (4%)
    all_to_all x1, waiting for transfers between devices, body(): lax.all_to_all(outgoing, 'post', split_axis=0, concat_axis=0, tiled=True)  76.8 us
    ppermute x7, waiting for transfers between devices, shift_in_plane(): return lax.ppermute(x, 'post', pairs)  16.7 us
    ppermute x9, starting transfers between devices, shift(): return lax.ppermute(x, axis, [(i, (i + k) % n) for i in range(n)])  16.3 us
    ppermute x9, waiting for transfers between devices, shift(): return lax.ppermute(x, axis, [(i, (i + k) % n) for i in range(n)])  9.62 us
    all_to_all x1, starting transfers between devices, body(): lax.all_to_all(copies, 'post', split_axis=0, concat_axis=0, tiled=True, a...  9.03 us
    all_to_all x1, starting transfers between devices, body(): lax.all_to_all(outgoing, 'post', split_axis=0, concat_axis=0, tiled=True)  7.66 us
    ppermute x7, starting transfers between devices, shift_in_plane(): return lax.ppermute(x, 'post', pairs)  6.94 us
    pallas_call x1, Pallas kernels, score(): pl.pallas_call(score_kernel, out_shape=jax.ShapeDtypeStruct((n_q, length)...  5.88 us
  transfers between devices with their start and end apart: 18, of which 11 were waited for; matrix products, arithmetic and copies ran while one was open for 4% of the time, Pallas kernels for 6%

profile of v2, /device:TPU:1, one launch (start us, length us, event | category | flops | bytes accessed | tf_op | source)
XLA Modules:
  0.0 178.1 jit_solution(4756053260330663379)
XLA Ops:
  0.6 3.9 %centroids.1 = (f32[64,256]{1,0:T(8,128)}, bf16[8,64,256]{2,1,0:T(8,128)(2,1)}) custom-call(s32[32]{0:T(128)} %lengths_hbm.3, s32[32,192]{1,0:T(8,128)} %labels_hbm.3, bf16[32,192,256]{2,1,0:T(8,128)(2,1)} %vectors_hbm.2), custom_call_target="tpu_custom_call" | custom-call | flops 100000000 | bytes 4194304 | tf_op jit(solution)/shard_map/centroids/pallas_call | solution.py:73
  4.5 9.0 %all-to-all-start = ((bf16[8,64,256]{2,1,0:T(8,128)(2,1)}), bf16[8,64,256]{2,1,0:T(8,128)(2,1)S(1)}, u32[]{:S(2)}, u32[]{:S(2)}) async-start(bf16[8,64,256]{2,1,0:T(8,128)(2,1)} %get-tuple-element.12), calls=%async_computation | async-start | bytes 524288 | tf_op jit(solution)/shard_map/all_to_all | solution.py:307
  13.6 5.0 %pack.1 = bf16[128,96,256]{2,1,0:T(8,128)(2,1)} custom-call(s32[2,32]{1,0:T(2,128)} %bitcast.51, s32[32]{0:T(128)} %lengths_hbm.3, s32[32,192]{1,0:T(8,128)} %labels_hbm.3, bf16[32,192,256]{2,1,0:T(8,128)(2,1)} %vectors_hbm.2), custom_call_target="tpu_custom_call" | custom-call | flops 1000000000 | bytes 16777216 | tf_op jit(solution)/shard_map/pack/pallas_call | solution.py:179
  18.5 5.4 %all-to-all-done = bf16[8,64,256]{2,1,0:T(8,128)(2,1)S(1)} async-done(((bf16[8,64,256]{2,1,0:T(8,128)(2,1)}), bf16[8,64,256]{2,1,0:T(8,128)(2,1)S(1)}, u32[]{:S(2)}, u32[]{:S(2)}) %all-to-all-start) | async-done | bytes 262176 | tf_op jit(solution)/shard_map/all_to_all | solution.py:307
  23.9 7.7 %all-to-all-start.1 = ((bf16[64,2,96,256]{3,2,1,0:T(8,128)(2,1)}), bf16[64,2,96,256]{3,2,1,0:T(8,128)(2,1)}, u32[]{:S(2)}, u32[]{:S(2)}) async-start(bf16[64,2,96,256]{3,2,1,0:T(8,128)(2,1)} %bitcast.42), calls=%async_computation.1 | async-start | bytes 12582912 | tf_op jit(solution)/shard_map/all_to_all | solution.py:317
  31.7 0.0 copy-start.6
  31.7 1.4 collective-permute-start.3
  33.1 2.6 %collective-permute-start.4 = (bf16[128,256]{1,0:T(8,128)(2,1)S(1)}, bf16[128,256]{1,0:T(8,128)(2,1)S(1)}, u32[]{:S(2)}, u32[]{:S(2)}) collective-permute-start(bf16[128,256]{1,0:T(8,128)(2,1)S(1)} %bitcast.46), channel_id=1, source_target_pairs={{0,2},{1,3},{2,0},{3,1},{4,6},{5,7},{6,4},{7,5},{8,10},{9,11},{10,... | collective-permute-start | bytes 196616 | tf_op jit(solution)/shard_map/ppermute | solution.py:276
  35.7 1.1 collective-permute-start.5
  36.7 0.0 collective-permute-done.3
  36.8 1.6 collective-permute-done.4
  38.3 0.9 collective-permute-done.5
  39.2 1.6 collective-permute-start.6
  40.8 1.5 collective-permute-start.7
  42.3 1.6 collective-permute-start.8
  43.9 0.2 collective-permute-start
  44.1 3.3 %collective-permute-start.1 = (bf16[8,192,256]{2,1,0:T(8,128)(2,1)S(1)}, bf16[8,192,256]{2,1,0:T(8,128)(2,1)S(1)}, u32[]{:S(2)}, u32[]{:S(2)}) collective-permute-start(bf16[8,192,256]{2,1,0:T(8,128)(2,1)S(1)} %copy-done), channel_id=1, source_target_pairs={{0,2},{1,3},{2,0},{3,1},{4,6},{5,7},{6,4},{7,5},{8,10},{9,11},{10,... | collective-permute-start | bytes 2359304 | tf_op jit(solution)/shard_map/ppermute | solution.py:276
  47.3 10.7 %collective-permute-done.6.refs_5_ = bf16[4,128,256]{2,1,0:T(8,128)(2,1)} collective-permute-done((bf16[4,128,256]{2,1,0:T(8,128)(2,1)S(1)}, bf16[4,128,256]{2,1,0:T(8,128)(2,1)}, u32[]{:S(2)}, u32[]{:S(2)}) %collective-permute-start.6) | collective-permute-done | bytes 262176 | tf_op jit(solution)/shard_map/ppermute | solution.py:285
  58.1 2.7 %collective-permute-start.2 = (bf16[8,192,256]{2,1,0:T(8,128)(2,1)S(1)}, bf16[8,192,256]{2,1,0:T(8,128)(2,1)S(1)}, u32[]{:S(2)}, u32[]{:S(2)}) collective-permute-start(bf16[8,192,256]{2,1,0:T(8,128)(2,1)S(1)} %copy-done), channel_id=1, source_target_pairs={{0,3},{1,0},{2,1},{3,2},{4,7},{5,4},{6,5},{7,6},{8,11},{9,8},{10,9... | collective-permute-start | bytes 2359304 | tf_op jit(solution)/shard_map/ppermute | solution.py:276
  60.8 0.0 collective-permute-done.7.refs_6_
  60.8 1.0 collective-permute-start.9
  61.8 5.7 %collective-permute-done.8.refs_7_ = bf16[4,128,256]{2,1,0:T(8,128)(2,1)S(1)} collective-permute-done((bf16[4,128,256]{2,1,0:T(8,128)(2,1)S(1)}, bf16[4,128,256]{2,1,0:T(8,128)(2,1)S(1)}, u32[]{:S(2)}, u32[]{:S(2)}) %collective-permute-start.8) | collective-permute-done | bytes 262176 | tf_op jit(solution)/shard_map/ppermute | solution.py:285
  67.5 0.7 copy-done.3
  68.2 0.7 collective-permute-start.10
  68.9 2.5 %constant_dynamic-slice_fusion = (s32[32,64]{0,1:T(8,128)}, s32[32,64]{0,1:T(8,128)}, s32[32,64]{0,1:T(8,128)}, s32[32,64]{0,1:T(8,128)}, s32[32,64]{0,1:T(8,128...) fusion(s32[2048,64]{0,1:T(8,128)} %param.12, ...), kind=kLoop, calls=%fused_computation.18 | loop fusion | bytes 262208 | tf_op jit(solution)/shard_map/dynamic_slice | solution.py:342
  71.4 1.2 concatenate.3
  72.6 0.0 collective-permute-done.9.refs_8_
  72.7 0.1 collective-permute-start.11
  72.8 0.5 collective-permute-start.12
  73.3 0.2 compare_reduce_fusion
  73.5 0.9 copy.12
  74.4 0.4 multiply_reduce_fusion
  74.7 0.2 collective-permute-done.12.refs_11_
  75.0 4.4 %collective-permute-done.1.refs_2_ = bf16[8,192,256]{2,1,0:T(8,128)(2,1)S(1)} collective-permute-done((bf16[8,192,256]{2,1,0:T(8,128)(2,1)S(1)}, bf16[8,192,256]{2,1,0:T(8,128)(2,1)S(1)}, u32[]{:S(2)}, u32[]{:S(2)}) %collective-permute-start.1) | collective-permute-done | bytes 786464 | tf_op jit(solution)/shard_map/ppermute | solution.py:276
  79.4 1.3 collective-permute-done.2.refs_3_
  80.7 1.1 broadcast_in_dim.5
  81.8 0.0 copy-start.5
  81.9 0.0 copy-start.7
  81.9 5.9 %score.1 = f32[8,192]{1,0:T(8,128)S(1)} custom-call(bf16[8,192,256]{2,1,0:T(8,128)(2,1)S(1)} %copy-done, bf16[8,192,256]{2,1,0:T(8,128)(2,1)S(1)} %collective-permute-done.refs_1_, bf16[8,192,256]{2,1,0:T(8,128)(2,1)S(1)} %collective-permute-done.1.refs_2_, bf16[8,192,256]{2,1,0:T(8,128)(2,1)S(1)} %collective-permute-done.2.refs_3_, ...), custom_call_target="tpu_custom_call" | custom-call | flops 4000000000 | bytes 6291456 | tf_op jit(solution)/shard_map/score/pallas_call | solution.py:226
  87.8 2.2 %collective-permute-start.13 = (f32[2,8,192]{2,1,0:T(8,128)S(1)}, f32[2,8,192]{2,1,0:T(8,128)S(1)}, u32[]{:S(2)}, u32[]{:S(2)}) collective-permute-start(f32[2,8,192]{2,1,0:T(8,128)S(1)} %pad_maximum_fusion.1), channel_id=1, source_target_pairs={{0,2},{1,3},{2,0},{3,1},{4,6},{5,7},{6,4},{7,5},{8,10},{9,11},{10,... | collective-permute-start | bytes 36872 | tf_op jit(solution)/shard_map/ppermute | solution.py:276
  89.9 1.9 %collective-permute-start.14 = (f32[2,8,192]{2,1,0:T(8,128)S(1)}, f32[2,8,192]{2,1,0:T(8,128)S(1)}, u32[]{:S(2)}, u32[]{:S(2)}) collective-permute-start(f32[2,8,192]{2,1,0:T(8,128)S(1)} %pad_maximum_fusion.1), channel_id=1, source_target_pairs={{0,1},{1,2},{2,3},{3,0},{4,5},{5,6},{6,7},{7,4},{8,9},{9,10},{10,1... | collective-permute-start | bytes 36872 | tf_op jit(solution)/shard_map/ppermute | solution.py:276
  91.8 1.0 collective-permute-start.15
  92.8 0.7 reshape.34
  93.5 0.8 collective-permute-done.14
  94.4 0.6 collective-permute-done.15
  95.0 0.7 fusion.4
  95.7 76.8 %all-to-all-done.1.got = bf16[64,2,96,256]{3,2,1,0:T(8,128)(2,1)} async-done(((bf16[64,2,96,256]{3,2,1,0:T(8,128)(2,1)}), bf16[64,2,96,256]{3,2,1,0:T(8,128)(2,1)}, u32[]{:S(2)}, u32[]{:S(2)}) %all-to-all-start.1) | async-done | bytes 6291488 | tf_op jit(solution)/shard_map/all_to_all | solution.py:317
  172.5 5.5 %store.1 = bf16[64,2,96,256]{3,2,1,0:T(8,128)(2,1)} custom-call(bf16[64,2,96,256]{3,2,1,0:T(8,128)(2,1)} %all-to-all-done.1.got), custom_call_target="tpu_custom_call" | custom-call | bytes 12582912 | tf_op jit(solution)/shard_map/store/pallas_call | solution.py:258
  (22 shorter events, 0.1 us)
Async XLA Ops:
  4.5 19.4 %all-to-all-start = ((bf16[8,64,256]{2,1,0:T(8,128)(2,1)}), bf16[8,64,256]{2,1,0:T(8,128)(2,1)S(1)}, u32[]{:S(2)}, u32[]{:S(2)}) async-start(bf16[8,64,256]{2,1,0:T(8,128)(2,1)} %get-tuple-element.12), calls=%async_computation | async-start | bytes 524288 | tf_op jit(solution)/shard_map/all_to_all | solution.py:307
  23.9 19.9 %copy-start = (bf16[8,192,256]{2,1,0:T(8,128)(2,1)S(1)}, bf16[8,192,256]{2,1,0:T(8,128)(2,1)}, u32[]{:S(2)}) copy-start(bf16[8,192,256]{2,1,0:T(8,128)(2,1)} %refs_0_) | copy-start | bytes 2359300
  23.9 148.6 %all-to-all-start.1 = ((bf16[64,2,96,256]{3,2,1,0:T(8,128)(2,1)}), bf16[64,2,96,256]{3,2,1,0:T(8,128)(2,1)}, u32[]{:S(2)}, u32[]{:S(2)}) async-start(bf16[64,2,96,256]{3,2,1,0:T(8,128)(2,1)} %bitcast.42), calls=%async_computation.1 | async-start | bytes 12582912 | tf_op jit(solution)/shard_map/all_to_all | solution.py:317
  31.7 42.7 %copy-start.6 = (bf16[8,256]{1,0:T(8,128)(2,1)S(1)}, bf16[8,256]{1,0:T(8,128)(2,1)}, u32[]{:S(2)}) copy-start(bf16[8,256]{1,0:T(8,128)(2,1)} %param.14) | copy-start | bytes 12292
  31.7 5.1 %collective-permute-start.3 = (bf16[128,256]{1,0:T(8,128)(2,1)S(1)}, bf16[128,256]{1,0:T(8,128)(2,1)S(1)}, u32[]{:S(2)}, u32[]{:S(2)}) collective-permute-start(bf16[128,256]{1,0:T(8,128)(2,1)S(1)} %bitcast.48), channel_id=1, source_target_pairs={{0,1},{1,2},{2,3},{3,0},{4,5},{5,6},{6,7},{7,4},{8,9},{9,10},{10,1... | collective-permute-start | bytes 196616 | tf_op jit(solution)/shard_map/ppermute | solution.py:276
  33.1 5.3 %collective-permute-start.4 = (bf16[128,256]{1,0:T(8,128)(2,1)S(1)}, bf16[128,256]{1,0:T(8,128)(2,1)S(1)}, u32[]{:S(2)}, u32[]{:S(2)}) collective-permute-start(bf16[128,256]{1,0:T(8,128)(2,1)S(1)} %bitcast.46), channel_id=1, source_target_pairs={{0,2},{1,3},{2,0},{3,1},{4,6},{5,7},{6,4},{7,5},{8,10},{9,11},{10,... | collective-permute-start | bytes 196616 | tf_op jit(solution)/shard_map/ppermute | solution.py:276
  35.7 3.5 %collective-permute-start.5 = (bf16[128,256]{1,0:T(8,128)(2,1)S(1)}, bf16[128,256]{1,0:T(8,128)(2,1)S(1)}, u32[]{:S(2)}, u32[]{:S(2)}) collective-permute-start(bf16[128,256]{1,0:T(8,128)(2,1)S(1)} %bitcast.45), channel_id=1, source_target_pairs={{0,3},{1,0},{2,1},{3,2},{4,7},{5,4},{6,5},{7,6},{8,11},{9,8},{10,9... | collective-permute-start | bytes 196616 | tf_op jit(solution)/shard_map/ppermute | solution.py:276
  39.2 18.8 %collective-permute-start.6 = (bf16[4,128,256]{2,1,0:T(8,128)(2,1)S(1)}, bf16[4,128,256]{2,1,0:T(8,128)(2,1)}, u32[]{:S(2)}, u32[]{:S(2)}) collective-permute-start(bf16[4,128,256]{2,1,0:T(8,128)(2,1)S(1)} %pad_maximum_fusion.refs_4_), channel_id=1, source_target_pairs={{0,64},{4,68},{8,72},{12,76},{16,80},{20,84},{24,88},{28,92},{32,9... | collective-permute-start | bytes 786440 | tf_op jit(solution)/shard_map/ppermute | solution.py:285
  40.8 20.0 %collective-permute-start.7 = (bf16[4,128,256]{2,1,0:T(8,128)(2,1)S(1)}, bf16[4,128,256]{2,1,0:T(8,128)(2,1)S(1)}, u32[]{:S(2)}, u32[]{:S(2)}) collective-permute-start(bf16[4,128,256]{2,1,0:T(8,128)(2,1)S(1)} %pad_maximum_fusion.refs_4_), channel_id=1, source_target_pairs={{0,192},{4,196},{8,200},{12,204},{16,208},{20,212},{24,216},{28,22... | collective-permute-start | bytes 786440 | tf_op jit(solution)/shard_map/ppermute | solution.py:285
  42.3 25.2 %collective-permute-start.8 = (bf16[4,128,256]{2,1,0:T(8,128)(2,1)S(1)}, bf16[4,128,256]{2,1,0:T(8,128)(2,1)S(1)}, u32[]{:S(2)}, u32[]{:S(2)}) collective-permute-start(bf16[4,128,256]{2,1,0:T(8,128)(2,1)S(1)} %pad_maximum_fusion.refs_4_), channel_id=1, source_target_pairs={{0,128},{4,132},{8,136},{12,140},{16,144},{20,148},{24,152},{28,15... | collective-permute-start | bytes 786440 | tf_op jit(solution)/shard_map/ppermute | solution.py:285
  43.9 31.1 %collective-permute-start = (bf16[8,192,256]{2,1,0:T(8,128)(2,1)S(1)}, bf16[8,192,256]{2,1,0:T(8,128)(2,1)S(1)}, u32[]{:S(2)}, u32[]{:S(2)}) collective-permute-start(bf16[8,192,256]{2,1,0:T(8,128)(2,1)S(1)} %copy-done), channel_id=1, source_target_pairs={{0,1},{1,2},{2,3},{3,0},{4,5},{5,6},{6,7},{7,4},{8,9},{9,10},{10,1... | collective-permute-start | bytes 2359304 | tf_op jit(solution)/shard_map/ppermute | solution.py:276
  44.1 35.3 %collective-permute-start.1 = (bf16[8,192,256]{2,1,0:T(8,128)(2,1)S(1)}, bf16[8,192,256]{2,1,0:T(8,128)(2,1)S(1)}, u32[]{:S(2)}, u32[]{:S(2)}) collective-permute-start(bf16[8,192,256]{2,1,0:T(8,128)(2,1)S(1)} %copy-done), channel_id=1, source_target_pairs={{0,2},{1,3},{2,0},{3,1},{4,6},{5,7},{6,4},{7,5},{8,10},{9,11},{10,... | collective-permute-start | bytes 2359304 | tf_op jit(solution)/shard_map/ppermute | solution.py:276
  58.1 22.6 %collective-permute-start.2 = (bf16[8,192,256]{2,1,0:T(8,128)(2,1)S(1)}, bf16[8,192,256]{2,1,0:T(8,128)(2,1)S(1)}, u32[]{:S(2)}, u32[]{:S(2)}) collective-permute-start(bf16[8,192,256]{2,1,0:T(8,128)(2,1)S(1)} %copy-done), channel_id=1, source_target_pairs={{0,3},{1,0},{2,1},{3,2},{4,7},{5,4},{6,5},{7,6},{8,11},{9,8},{10,9... | collective-permute-start | bytes 2359304 | tf_op jit(solution)/shard_map/ppermute | solution.py:276
  60.8 6.7 %copy-start.1 = (bf16[4,128,256]{2,1,0:T(8,128)(2,1)}, bf16[4,128,256]{2,1,0:T(8,128)(2,1)S(1)}, u32[]{:S(2)}) copy-start(bf16[4,128,256]{2,1,0:T(8,128)(2,1)S(1)} %collective-permute-done.7.refs_6_) | copy-start | bytes 786436
  60.8 11.8 %collective-permute-start.9 = (bf16[4,128,256]{2,1,0:T(8,128)(2,1)S(1)}, bf16[4,128,256]{2,1,0:T(8,128)(2,1)}, u32[]{:S(2)}, u32[]{:S(2)}) collective-permute-start(bf16[4,128,256]{2,1,0:T(8,128)(2,1)S(1)} %pad_maximum_fusion.refs_4_), channel_id=1, source_target_pairs={{0,4},{4,0},{8,12},{12,8},{16,20},{20,16},{24,28},{28,24},{32,36},... | collective-permute-start | bytes 786440 | tf_op jit(solution)/shard_map/ppermute | solution.py:285
  67.5 0.7 copy-start.3
  68.2 4.6 %collective-permute-start.10 = (bf16[4,128,256]{2,1,0:T(8,128)(2,1)}, bf16[4,128,256]{2,1,0:T(8,128)(2,1)}, u32[]{:S(2)}, u32[]{:S(2)}) collective-permute-start(bf16[4,128,256]{2,1,0:T(8,128)(2,1)} %collective-permute-done.6.refs_5_), channel_id=1, source_target_pairs={{0,4},{4,0},{8,12},{12,8},{16,20},{20,16},{24,28},{28,24},{32,36},... | collective-permute-start | bytes 786440 | tf_op jit(solution)/shard_map/ppermute | solution.py:285
  72.7 2.1 %collective-permute-start.11 = (bf16[4,128,256]{2,1,0:T(8,128)(2,1)}, bf16[4,128,256]{2,1,0:T(8,128)(2,1)}, u32[]{:S(2)}, u32[]{:S(2)}) collective-permute-start(bf16[4,128,256]{2,1,0:T(8,128)(2,1)} %copy-done.1), channel_id=1, source_target_pairs={{0,4},{4,0},{8,12},{12,8},{16,20},{20,16},{24,28},{28,24},{32,36},... | collective-permute-start | bytes 786440 | tf_op jit(solution)/shard_map/ppermute | solution.py:285
  72.8 2.2 %collective-permute-start.12 = (bf16[4,128,256]{2,1,0:T(8,128)(2,1)}, bf16[4,128,256]{2,1,0:T(8,128)(2,1)}, u32[]{:S(2)}, u32[]{:S(2)}) collective-permute-start(bf16[4,128,256]{2,1,0:T(8,128)(2,1)} %copy-done.3), channel_id=1, source_target_pairs={{0,4},{4,0},{8,12},{12,8},{16,20},{20,16},{24,28},{28,24},{32,36},... | collective-permute-start | bytes 786440 | tf_op jit(solution)/shard_map/ppermute | solution.py:285
  74.4 7.5 %copy-start.2 = (bf16[4,128,256]{2,1,0:T(8,128)(2,1)S(1)}, bf16[4,128,256]{2,1,0:T(8,128)(2,1)}, u32[]{:S(2)}) copy-start(bf16[4,128,256]{2,1,0:T(8,128)(2,1)} %copy-done.1) | copy-start | bytes 786436
  74.4 7.5 %copy-start.4 = (bf16[4,128,256]{2,1,0:T(8,128)(2,1)S(1)}, bf16[4,128,256]{2,1,0:T(8,128)(2,1)}, u32[]{:S(2)}) copy-start(bf16[4,128,256]{2,1,0:T(8,128)(2,1)} %copy-done.3) | copy-start | bytes 786436
  81.8 11.0 %copy-start.5 = (f32[64,256]{1,0:T(8,128)S(1)}, f32[64,256]{1,0:T(8,128)}, u32[]{:S(2)}) copy-start(f32[64,256]{1,0:T(8,128)} %get-tuple-element.16) | copy-start | bytes 196612
  81.9 13.1 %copy-start.7 = (s32[8]{0:T(128)S(1)}, s32[8]{0:T(128)}, u32[]{:S(2)}) copy-start(s32[8]{0:T(128)} %param.15) | copy-start | bytes 100
  87.8 5.7 %collective-permute-start.13 = (f32[2,8,192]{2,1,0:T(8,128)S(1)}, f32[2,8,192]{2,1,0:T(8,128)S(1)}, u32[]{:S(2)}, u32[]{:S(2)}) collective-permute-start(f32[2,8,192]{2,1,0:T(8,128)S(1)} %pad_maximum_fusion.1), channel_id=1, source_target_pairs={{0,2},{1,3},{2,0},{3,1},{4,6},{5,7},{6,4},{7,5},{8,10},{9,11},{10,... | collective-permute-start | bytes 36872 | tf_op jit(solution)/shard_map/ppermute | solution.py:276
  89.9 4.4 %collective-permute-start.14 = (f32[2,8,192]{2,1,0:T(8,128)S(1)}, f32[2,8,192]{2,1,0:T(8,128)S(1)}, u32[]{:S(2)}, u32[]{:S(2)}) collective-permute-start(f32[2,8,192]{2,1,0:T(8,128)S(1)} %pad_maximum_fusion.1), channel_id=1, source_target_pairs={{0,1},{1,2},{2,3},{3,0},{4,5},{5,6},{6,7},{7,4},{8,9},{9,10},{10,1... | collective-permute-start | bytes 36872 | tf_op jit(solution)/shard_map/ppermute | solution.py:276
  91.8 3.1 %collective-permute-start.15 = (f32[2,8,192]{2,1,0:T(8,128)S(1)}, f32[2,8,192]{2,1,0:T(8,128)S(1)}, u32[]{:S(2)}, u32[]{:S(2)}) collective-permute-start(f32[2,8,192]{2,1,0:T(8,128)S(1)} %pad_maximum_fusion.1), channel_id=1, source_target_pairs={{0,3},{1,0},{2,1},{3,2},{4,7},{5,4},{6,5},{7,6},{8,11},{9,8},{10,9... | collective-permute-start | bytes 36872 | tf_op jit(solution)/shard_map/ppermute | solution.py:276

commit v3 on v2

--- a/solution.py
+++ b/solution.py
@@ -16,7 +16,7 @@
 def centroid_kernel(lengths_hbm, labels_hbm, vectors_hbm, cents_ref, copies_ref,
                     lengths_vec, labels_ref, vectors_ref, sums_ref, half_ref, small_sem, in_sem):
     s_local, length = labels_ref.shape
-    group = 4
+    group = 8
     n_group = s_local // group
 
     def fetch(g):
@@ -41,17 +41,18 @@
         jnp.where(same, lengths_vec[...].astype(jnp.float32), 0.0), axis=1, keepdims=True
     )
     row_id = lax.broadcasted_iota(jnp.int32, (s_local, length), 1).astype(jnp.float32)
-    half_ref[...] = jnp.where(row_id < lengths, labels_ref[...], 2)
+    half_ref[...] = jnp.where(row_id < lengths, labels_ref[...], -100)
     sum_id = lax.broadcasted_iota(jnp.int32, (16, length), 0)
     for g in range(n_group):
         fetch(g).wait()
-        sums = []
-        for s in range(g * group, (g + 1) * group):
-            member = jnp.where(half_ref[s : s + 1, :] == sum_id, 1.0, 0.0).astype(jnp.bfloat16)
-            sums.append(
-                jnp.dot(member, vectors_ref[s], preferred_element_type=jnp.float32)[:2]
+        total = 0.0
+        for j in range(group):
+            s = g * group + j
+            member = jnp.where(half_ref[s : s + 1, :] + 2 * j == sum_id, 1.0, 0.0)
+            total += jnp.dot(
+                member.astype(jnp.bfloat16), vectors_ref[s], preferred_element_type=jnp.float32
             )
-        sums_ref[g * 8 : g * 8 + 8, :] = jnp.concatenate(sums, axis=0)
+        sums_ref[g * 2 * group : (g + 1) * 2 * group, :] = total[: 2 * group]
 
     which = lax.broadcasted_iota(jnp.int32, (2 * s_local, s_local), 0)
     split_id = lax.broadcasted_iota(jnp.int32, (2 * s_local, s_local), 1)
@@ -85,7 +86,7 @@
             pltpu.VMEM((2 * s_local, dims), jnp.float32),
             pltpu.VMEM((s_local, length), jnp.int32),
             pltpu.SemaphoreType.DMA((2,)),
-            pltpu.SemaphoreType.DMA((s_local // 4,)),
+            pltpu.SemaphoreType.DMA((s_local // 8,)),
         ],
         compiler_params=pltpu.CompilerParams(vmem_limit_bytes=56 << 20),
         cost_estimate=pl.CostEstimate(flops=10**8, bytes_accessed=4 << 20, transcendentals=0),
@@ -254,7 +255,7 @@
 
 
 def store(got):
-    n_copies = 16
+    n_copies = 4
     return pl.pallas_call(
         store_kernel,
         out_shape=jax.ShapeDtypeStruct(got.shape, got.dtype),

time: 179 us -> 178 us (level)
  no operation moved by 1% of the time
where the time goes in v3:
time: 178 us
  waiting for transfers between devices  109 us (61%)
  starting transfers between devices  40 us (22%)
  Pallas kernels  19.6 us (11%)
  local copies, waits for them, and re-layouts  7.12 us (4%)
    all_to_all x1, waiting for transfers between devices, body(): lax.all_to_all(outgoing, 'post', split_axis=0, concat_axis=0, tiled=True)  76.8 us
    ppermute x7, waiting for transfers between devices, shift_in_plane(): return lax.ppermute(x, 'post', pairs)  16.7 us
    ppermute x9, starting transfers between devices, shift(): return lax.ppermute(x, axis, [(i, (i + k) % n) for i in range(n)])  16.3 us
    ppermute x9, waiting for transfers between devices, shift(): return lax.ppermute(x, axis, [(i, (i + k) % n) for i in range(n)])  9.62 us
    all_to_all x1, starting transfers between devices, body(): lax.all_to_all(copies, 'post', split_axis=0, concat_axis=0, tiled=True, a...  9.03 us
    all_to_all x1, starting transfers between devices, body(): lax.all_to_all(outgoing, 'post', split_axis=0, concat_axis=0, tiled=True)  7.66 us
    ppermute x7, starting transfers between devices, shift_in_plane(): return lax.ppermute(x, 'post', pairs)  6.94 us
    pallas_call x1, Pallas kernels, score(): pl.pallas_call(score_kernel, out_shape=jax.ShapeDtypeStruct((n_q, length)...  5.88 us
  transfers between devices with their start and end apart: 18, of which 11 were waited for; matrix products, arithmetic and copies ran while one was open for 4% of the time, Pallas kernels for 6%

profile of v3, /device:TPU:1, one launch (start us, length us, event | category | flops | bytes accessed | tf_op | source)
XLA Modules:
  0.0 177.6 jit_solution(12095699047468919676)
XLA Ops:
  0.6 3.6 %centroids.1 = (f32[64,256]{1,0:T(8,128)}, bf16[8,64,256]{2,1,0:T(8,128)(2,1)}) custom-call(s32[32]{0:T(128)} %lengths_hbm.3, s32[32,192]{1,0:T(8,128)} %labels_hbm.3, bf16[32,192,256]{2,1,0:T(8,128)(2,1)} %vectors_hbm.2), custom_call_target="tpu_custom_call" | custom-call | flops 100000000 | bytes 4194304 | tf_op jit(solution)/shard_map/centroids/pallas_call | solution.py:74
  4.3 9.0 %all-to-all-start = ((bf16[8,64,256]{2,1,0:T(8,128)(2,1)}), bf16[8,64,256]{2,1,0:T(8,128)(2,1)S(1)}, u32[]{:S(2)}, u32[]{:S(2)}) async-start(bf16[8,64,256]{2,1,0:T(8,128)(2,1)} %get-tuple-element.12), calls=%async_computation | async-start | bytes 524288 | tf_op jit(solution)/shard_map/all_to_all | solution.py:308
  13.3 4.9 %pack.1 = bf16[128,96,256]{2,1,0:T(8,128)(2,1)} custom-call(s32[2,32]{1,0:T(2,128)} %bitcast.51, s32[32]{0:T(128)} %lengths_hbm.3, s32[32,192]{1,0:T(8,128)} %labels_hbm.3, bf16[32,192,256]{2,1,0:T(8,128)(2,1)} %vectors_hbm.2), custom_call_target="tpu_custom_call" | custom-call | flops 1000000000 | bytes 16777216 | tf_op jit(solution)/shard_map/pack/pallas_call | solution.py:180
  18.2 5.5 %all-to-all-done = bf16[8,64,256]{2,1,0:T(8,128)(2,1)S(1)} async-done(((bf16[8,64,256]{2,1,0:T(8,128)(2,1)}), bf16[8,64,256]{2,1,0:T(8,128)(2,1)S(1)}, u32[]{:S(2)}, u32[]{:S(2)}) %all-to-all-start) | async-done | bytes 262176 | tf_op jit(solution)/shard_map/all_to_all | solution.py:308
  23.7 7.7 %all-to-all-start.1 = ((bf16[64,2,96,256]{3,2,1,0:T(8,128)(2,1)}), bf16[64,2,96,256]{3,2,1,0:T(8,128)(2,1)}, u32[]{:S(2)}, u32[]{:S(2)}) async-start(bf16[64,2,96,256]{3,2,1,0:T(8,128)(2,1)} %bitcast.42), calls=%async_computation.1 | async-start | bytes 12582912 | tf_op jit(solution)/shard_map/all_to_all | solution.py:318
  31.4 0.0 copy-start.6
  31.4 1.4 collective-permute-start.3
  32.8 2.6 %collective-permute-start.4 = (bf16[128,256]{1,0:T(8,128)(2,1)S(1)}, bf16[128,256]{1,0:T(8,128)(2,1)S(1)}, u32[]{:S(2)}, u32[]{:S(2)}) collective-permute-start(bf16[128,256]{1,0:T(8,128)(2,1)S(1)} %bitcast.46), channel_id=1, source_target_pairs={{0,2},{1,3},{2,0},{3,1},{4,6},{5,7},{6,4},{7,5},{8,10},{9,11},{10,... | collective-permute-start | bytes 196616 | tf_op jit(solution)/shard_map/ppermute | solution.py:277
  35.4 1.1 collective-permute-start.5
  36.5 0.0 collective-permute-done.3
  36.5 1.6 collective-permute-done.4
  38.1 0.9 collective-permute-done.5
  39.0 1.6 collective-permute-start.6
  40.5 1.5 collective-permute-start.7
  42.1 1.6 collective-permute-start.8
  43.6 0.2 collective-permute-start
  43.8 3.3 %collective-permute-start.1 = (bf16[8,192,256]{2,1,0:T(8,128)(2,1)S(1)}, bf16[8,192,256]{2,1,0:T(8,128)(2,1)S(1)}, u32[]{:S(2)}, u32[]{:S(2)}) collective-permute-start(bf16[8,192,256]{2,1,0:T(8,128)(2,1)S(1)} %copy-done), channel_id=1, source_target_pairs={{0,2},{1,3},{2,0},{3,1},{4,6},{5,7},{6,4},{7,5},{8,10},{9,11},{10,... | collective-permute-start | bytes 2359304 | tf_op jit(solution)/shard_map/ppermute | solution.py:277
  47.1 10.7 %collective-permute-done.6.refs_5_ = bf16[4,128,256]{2,1,0:T(8,128)(2,1)} collective-permute-done((bf16[4,128,256]{2,1,0:T(8,128)(2,1)S(1)}, bf16[4,128,256]{2,1,0:T(8,128)(2,1)}, u32[]{:S(2)}, u32[]{:S(2)}) %collective-permute-start.6) | collective-permute-done | bytes 262176 | tf_op jit(solution)/shard_map/ppermute | solution.py:286
  57.8 2.7 %collective-permute-start.2 = (bf16[8,192,256]{2,1,0:T(8,128)(2,1)S(1)}, bf16[8,192,256]{2,1,0:T(8,128)(2,1)S(1)}, u32[]{:S(2)}, u32[]{:S(2)}) collective-permute-start(bf16[8,192,256]{2,1,0:T(8,128)(2,1)S(1)} %copy-done), channel_id=1, source_target_pairs={{0,3},{1,0},{2,1},{3,2},{4,7},{5,4},{6,5},{7,6},{8,11},{9,8},{10,9... | collective-permute-start | bytes 2359304 | tf_op jit(solution)/shard_map/ppermute | solution.py:277
  60.6 1.0 collective-permute-start.9
  61.5 5.7 %collective-permute-done.8.refs_7_ = bf16[4,128,256]{2,1,0:T(8,128)(2,1)S(1)} collective-permute-done((bf16[4,128,256]{2,1,0:T(8,128)(2,1)S(1)}, bf16[4,128,256]{2,1,0:T(8,128)(2,1)S(1)}, u32[]{:S(2)}, u32[]{:S(2)}) %collective-permute-start.8) | collective-permute-done | bytes 262176 | tf_op jit(solution)/shard_map/ppermute | solution.py:286
  67.2 0.7 copy-done.3
  67.9 0.7 collective-permute-start.10
  68.7 2.5 %constant_dynamic-slice_fusion = (s32[32,64]{0,1:T(8,128)}, s32[32,64]{0,1:T(8,128)}, s32[32,64]{0,1:T(8,128)}, s32[32,64]{0,1:T(8,128)}, s32[32,64]{0,1:T(8,128...) fusion(s32[2048,64]{0,1:T(8,128)} %param.12, ...), kind=kLoop, calls=%fused_computation.18 | loop fusion | bytes 262208 | tf_op jit(solution)/shard_map/dynamic_slice | solution.py:343
  71.2 1.2 concatenate.3
  72.4 0.0 collective-permute-done.9.refs_8_
  72.4 0.1 collective-permute-start.11
  72.5 0.0 collective-permute-done.10.refs_9_
  72.5 0.5 collective-permute-start.12
  73.0 0.2 compare_reduce_fusion
  73.2 0.9 copy.12
  74.1 0.4 multiply_reduce_fusion
  74.5 0.2 collective-permute-done.12.refs_11_
  74.7 4.4 %collective-permute-done.1.refs_2_ = bf16[8,192,256]{2,1,0:T(8,128)(2,1)S(1)} collective-permute-done((bf16[8,192,256]{2,1,0:T(8,128)(2,1)S(1)}, bf16[8,192,256]{2,1,0:T(8,128)(2,1)S(1)}, u32[]{:S(2)}, u32[]{:S(2)}) %collective-permute-start.1) | collective-permute-done | bytes 786464 | tf_op jit(solution)/shard_map/ppermute | solution.py:277
  79.1 1.3 collective-permute-done.2.refs_3_
  80.4 1.1 broadcast_in_dim.5
  81.6 0.0 copy-start.5
  81.6 0.0 copy-start.7
  81.6 5.9 %score.1 = f32[8,192]{1,0:T(8,128)S(1)} custom-call(bf16[8,192,256]{2,1,0:T(8,128)(2,1)S(1)} %copy-done, bf16[8,192,256]{2,1,0:T(8,128)(2,1)S(1)} %collective-permute-done.refs_1_, bf16[8,192,256]{2,1,0:T(8,128)(2,1)S(1)} %collective-permute-done.1.refs_2_, bf16[8,192,256]{2,1,0:T(8,128)(2,1)S(1)} %collective-permute-done.2.refs_3_, ...), custom_call_target="tpu_custom_call" | custom-call | flops 4000000000 | bytes 6291456 | tf_op jit(solution)/shard_map/score/pallas_call | solution.py:227
  87.5 2.2 %collective-permute-start.13 = (f32[2,8,192]{2,1,0:T(8,128)S(1)}, f32[2,8,192]{2,1,0:T(8,128)S(1)}, u32[]{:S(2)}, u32[]{:S(2)}) collective-permute-start(f32[2,8,192]{2,1,0:T(8,128)S(1)} %pad_maximum_fusion.1), channel_id=1, source_target_pairs={{0,2},{1,3},{2,0},{3,1},{4,6},{5,7},{6,4},{7,5},{8,10},{9,11},{10,... | collective-permute-start | bytes 36872 | tf_op jit(solution)/shard_map/ppermute | solution.py:277
  89.7 1.9 %collective-permute-start.14 = (f32[2,8,192]{2,1,0:T(8,128)S(1)}, f32[2,8,192]{2,1,0:T(8,128)S(1)}, u32[]{:S(2)}, u32[]{:S(2)}) collective-permute-start(f32[2,8,192]{2,1,0:T(8,128)S(1)} %pad_maximum_fusion.1), channel_id=1, source_target_pairs={{0,1},{1,2},{2,3},{3,0},{4,5},{5,6},{6,7},{7,4},{8,9},{9,10},{10,1... | collective-permute-start | bytes 36872 | tf_op jit(solution)/shard_map/ppermute | solution.py:277
  91.6 1.0 collective-permute-start.15
  92.6 0.7 reshape.34
  93.3 0.8 collective-permute-done.14
  94.1 0.6 collective-permute-done.15
  94.7 0.7 fusion.4
  95.4 76.8 %all-to-all-done.1.got = bf16[64,2,96,256]{3,2,1,0:T(8,128)(2,1)} async-done(((bf16[64,2,96,256]{3,2,1,0:T(8,128)(2,1)}), bf16[64,2,96,256]{3,2,1,0:T(8,128)(2,1)}, u32[]{:S(2)}, u32[]{:S(2)}) %all-to-all-start.1) | async-done | bytes 6291488 | tf_op jit(solution)/shard_map/all_to_all | solution.py:318
  172.3 5.2 %store.1 = bf16[64,2,96,256]{3,2,1,0:T(8,128)(2,1)} custom-call(bf16[64,2,96,256]{3,2,1,0:T(8,128)(2,1)} %all-to-all-done.1.got), custom_call_target="tpu_custom_call" | custom-call | bytes 12582912 | tf_op jit(solution)/shard_map/store/pallas_call | solution.py:259
  (22 shorter events, 0.1 us)
Async XLA Ops:
  4.3 19.4 %all-to-all-start = ((bf16[8,64,256]{2,1,0:T(8,128)(2,1)}), bf16[8,64,256]{2,1,0:T(8,128)(2,1)S(1)}, u32[]{:S(2)}, u32[]{:S(2)}) async-start(bf16[8,64,256]{2,1,0:T(8,128)(2,1)} %get-tuple-element.12), calls=%async_computation | async-start | bytes 524288 | tf_op jit(solution)/shard_map/all_to_all | solution.py:308
  23.7 19.9 %copy-start = (bf16[8,192,256]{2,1,0:T(8,128)(2,1)S(1)}, bf16[8,192,256]{2,1,0:T(8,128)(2,1)}, u32[]{:S(2)}) copy-start(bf16[8,192,256]{2,1,0:T(8,128)(2,1)} %refs_0_) | copy-start | bytes 2359300
  23.7 148.6 %all-to-all-start.1 = ((bf16[64,2,96,256]{3,2,1,0:T(8,128)(2,1)}), bf16[64,2,96,256]{3,2,1,0:T(8,128)(2,1)}, u32[]{:S(2)}, u32[]{:S(2)}) async-start(bf16[64,2,96,256]{3,2,1,0:T(8,128)(2,1)} %bitcast.42), calls=%async_computation.1 | async-start | bytes 12582912 | tf_op jit(solution)/shard_map/all_to_all | solution.py:318
  31.4 42.7 %copy-start.6 = (bf16[8,256]{1,0:T(8,128)(2,1)S(1)}, bf16[8,256]{1,0:T(8,128)(2,1)}, u32[]{:S(2)}) copy-start(bf16[8,256]{1,0:T(8,128)(2,1)} %param.14) | copy-start | bytes 12292
  31.4 5.1 %collective-permute-start.3 = (bf16[128,256]{1,0:T(8,128)(2,1)S(1)}, bf16[128,256]{1,0:T(8,128)(2,1)S(1)}, u32[]{:S(2)}, u32[]{:S(2)}) collective-permute-start(bf16[128,256]{1,0:T(8,128)(2,1)S(1)} %bitcast.48), channel_id=1, source_target_pairs={{0,1},{1,2},{2,3},{3,0},{4,5},{5,6},{6,7},{7,4},{8,9},{9,10},{10,1... | collective-permute-start | bytes 196616 | tf_op jit(solution)/shard_map/ppermute | solution.py:277
  32.8 5.3 %collective-permute-start.4 = (bf16[128,256]{1,0:T(8,128)(2,1)S(1)}, bf16[128,256]{1,0:T(8,128)(2,1)S(1)}, u32[]{:S(2)}, u32[]{:S(2)}) collective-permute-start(bf16[128,256]{1,0:T(8,128)(2,1)S(1)} %bitcast.46), channel_id=1, source_target_pairs={{0,2},{1,3},{2,0},{3,1},{4,6},{5,7},{6,4},{7,5},{8,10},{9,11},{10,... | collective-permute-start | bytes 196616 | tf_op jit(solution)/shard_map/ppermute | solution.py:277
  35.4 3.5 %collective-permute-start.5 = (bf16[128,256]{1,0:T(8,128)(2,1)S(1)}, bf16[128,256]{1,0:T(8,128)(2,1)S(1)}, u32[]{:S(2)}, u32[]{:S(2)}) collective-permute-start(bf16[128,256]{1,0:T(8,128)(2,1)S(1)} %bitcast.45), channel_id=1, source_target_pairs={{0,3},{1,0},{2,1},{3,2},{4,7},{5,4},{6,5},{7,6},{8,11},{9,8},{10,9... | collective-permute-start | bytes 196616 | tf_op jit(solution)/shard_map/ppermute | solution.py:277
  39.0 18.8 %collective-permute-start.6 = (bf16[4,128,256]{2,1,0:T(8,128)(2,1)S(1)}, bf16[4,128,256]{2,1,0:T(8,128)(2,1)}, u32[]{:S(2)}, u32[]{:S(2)}) collective-permute-start(bf16[4,128,256]{2,1,0:T(8,128)(2,1)S(1)} %pad_maximum_fusion.refs_4_), channel_id=1, source_target_pairs={{0,64},{4,68},{8,72},{12,76},{16,80},{20,84},{24,88},{28,92},{32,9... | collective-permute-start | bytes 786440 | tf_op jit(solution)/shard_map/ppermute | solution.py:286
  40.5 20.0 %collective-permute-start.7 = (bf16[4,128,256]{2,1,0:T(8,128)(2,1)S(1)}, bf16[4,128,256]{2,1,0:T(8,128)(2,1)S(1)}, u32[]{:S(2)}, u32[]{:S(2)}) collective-permute-start(bf16[4,128,256]{2,1,0:T(8,128)(2,1)S(1)} %pad_maximum_fusion.refs_4_), channel_id=1, source_target_pairs={{0,192},{4,196},{8,200},{12,204},{16,208},{20,212},{24,216},{28,22... | collective-permute-start | bytes 786440 | tf_op jit(solution)/shard_map/ppermute | solution.py:286
  42.1 25.2 %collective-permute-start.8 = (bf16[4,128,256]{2,1,0:T(8,128)(2,1)S(1)}, bf16[4,128,256]{2,1,0:T(8,128)(2,1)S(1)}, u32[]{:S(2)}, u32[]{:S(2)}) collective-permute-start(bf16[4,128,256]{2,1,0:T(8,128)(2,1)S(1)} %pad_maximum_fusion.refs_4_), channel_id=1, source_target_pairs={{0,128},{4,132},{8,136},{12,140},{16,144},{20,148},{24,152},{28,15... | collective-permute-start | bytes 786440 | tf_op jit(solution)/shard_map/ppermute | solution.py:286
  43.6 31.1 %collective-permute-start = (bf16[8,192,256]{2,1,0:T(8,128)(2,1)S(1)}, bf16[8,192,256]{2,1,0:T(8,128)(2,1)S(1)}, u32[]{:S(2)}, u32[]{:S(2)}) collective-permute-start(bf16[8,192,256]{2,1,0:T(8,128)(2,1)S(1)} %copy-done), channel_id=1, source_target_pairs={{0,1},{1,2},{2,3},{3,0},{4,5},{5,6},{6,7},{7,4},{8,9},{9,10},{10,1... | collective-permute-start | bytes 2359304 | tf_op jit(solution)/shard_map/ppermute | solution.py:277
  43.8 35.3 %collective-permute-start.1 = (bf16[8,192,256]{2,1,0:T(8,128)(2,1)S(1)}, bf16[8,192,256]{2,1,0:T(8,128)(2,1)S(1)}, u32[]{:S(2)}, u32[]{:S(2)}) collective-permute-start(bf16[8,192,256]{2,1,0:T(8,128)(2,1)S(1)} %copy-done), channel_id=1, source_target_pairs={{0,2},{1,3},{2,0},{3,1},{4,6},{5,7},{6,4},{7,5},{8,10},{9,11},{10,... | collective-permute-start | bytes 2359304 | tf_op jit(solution)/shard_map/ppermute | solution.py:277
  57.8 22.6 %collective-permute-start.2 = (bf16[8,192,256]{2,1,0:T(8,128)(2,1)S(1)}, bf16[8,192,256]{2,1,0:T(8,128)(2,1)S(1)}, u32[]{:S(2)}, u32[]{:S(2)}) collective-permute-start(bf16[8,192,256]{2,1,0:T(8,128)(2,1)S(1)} %copy-done), channel_id=1, source_target_pairs={{0,3},{1,0},{2,1},{3,2},{4,7},{5,4},{6,5},{7,6},{8,11},{9,8},{10,9... | collective-permute-start | bytes 2359304 | tf_op jit(solution)/shard_map/ppermute | solution.py:277
  60.6 6.7 %copy-start.1 = (bf16[4,128,256]{2,1,0:T(8,128)(2,1)}, bf16[4,128,256]{2,1,0:T(8,128)(2,1)S(1)}, u32[]{:S(2)}) copy-start(bf16[4,128,256]{2,1,0:T(8,128)(2,1)S(1)} %collective-permute-done.7.refs_6_) | copy-start | bytes 786436
  60.6 11.8 %collective-permute-start.9 = (bf16[4,128,256]{2,1,0:T(8,128)(2,1)S(1)}, bf16[4,128,256]{2,1,0:T(8,128)(2,1)}, u32[]{:S(2)}, u32[]{:S(2)}) collective-permute-start(bf16[4,128,256]{2,1,0:T(8,128)(2,1)S(1)} %pad_maximum_fusion.refs_4_), channel_id=1, source_target_pairs={{0,4},{4,0},{8,12},{12,8},{16,20},{20,16},{24,28},{28,24},{32,36},... | collective-permute-start | bytes 786440 | tf_op jit(solution)/shard_map/ppermute | solution.py:286
  67.2 0.7 copy-start.3
  67.9 4.6 %collective-permute-start.10 = (bf16[4,128,256]{2,1,0:T(8,128)(2,1)}, bf16[4,128,256]{2,1,0:T(8,128)(2,1)}, u32[]{:S(2)}, u32[]{:S(2)}) collective-permute-start(bf16[4,128,256]{2,1,0:T(8,128)(2,1)} %collective-permute-done.6.refs_5_), channel_id=1, source_target_pairs={{0,4},{4,0},{8,12},{12,8},{16,20},{20,16},{24,28},{28,24},{32,36},... | collective-permute-start | bytes 786440 | tf_op jit(solution)/shard_map/ppermute | solution.py:286
  72.4 2.1 %collective-permute-start.11 = (bf16[4,128,256]{2,1,0:T(8,128)(2,1)}, bf16[4,128,256]{2,1,0:T(8,128)(2,1)}, u32[]{:S(2)}, u32[]{:S(2)}) collective-permute-start(bf16[4,128,256]{2,1,0:T(8,128)(2,1)} %copy-done.1), channel_id=1, source_target_pairs={{0,4},{4,0},{8,12},{12,8},{16,20},{20,16},{24,28},{28,24},{32,36},... | collective-permute-start | bytes 786440 | tf_op jit(solution)/shard_map/ppermute | solution.py:286
  72.5 2.2 %collective-permute-start.12 = (bf16[4,128,256]{2,1,0:T(8,128)(2,1)}, bf16[4,128,256]{2,1,0:T(8,128)(2,1)}, u32[]{:S(2)}, u32[]{:S(2)}) collective-permute-start(bf16[4,128,256]{2,1,0:T(8,128)(2,1)} %copy-done.3), channel_id=1, source_target_pairs={{0,4},{4,0},{8,12},{12,8},{16,20},{20,16},{24,28},{28,24},{32,36},... | collective-permute-start | bytes 786440 | tf_op jit(solution)/shard_map/ppermute | solution.py:286
  74.1 7.5 %copy-start.2 = (bf16[4,128,256]{2,1,0:T(8,128)(2,1)S(1)}, bf16[4,128,256]{2,1,0:T(8,128)(2,1)}, u32[]{:S(2)}) copy-start(bf16[4,128,256]{2,1,0:T(8,128)(2,1)} %copy-done.1) | copy-start | bytes 786436
  74.1 7.5 %copy-start.4 = (bf16[4,128,256]{2,1,0:T(8,128)(2,1)S(1)}, bf16[4,128,256]{2,1,0:T(8,128)(2,1)}, u32[]{:S(2)}) copy-start(bf16[4,128,256]{2,1,0:T(8,128)(2,1)} %copy-done.3) | copy-start | bytes 786436
  81.6 11.0 %copy-start.5 = (f32[64,256]{1,0:T(8,128)S(1)}, f32[64,256]{1,0:T(8,128)}, u32[]{:S(2)}) copy-start(f32[64,256]{1,0:T(8,128)} %get-tuple-element.16) | copy-start | bytes 196612
  81.6 13.1 %copy-start.7 = (s32[8]{0:T(128)S(1)}, s32[8]{0:T(128)}, u32[]{:S(2)}) copy-start(s32[8]{0:T(128)} %param.15) | copy-start | bytes 100
  87.5 5.7 %collective-permute-start.13 = (f32[2,8,192]{2,1,0:T(8,128)S(1)}, f32[2,8,192]{2,1,0:T(8,128)S(1)}, u32[]{:S(2)}, u32[]{:S(2)}) collective-permute-start(f32[2,8,192]{2,1,0:T(8,128)S(1)} %pad_maximum_fusion.1), channel_id=1, source_target_pairs={{0,2},{1,3},{2,0},{3,1},{4,6},{5,7},{6,4},{7,5},{8,10},{9,11},{10,... | collective-permute-start | bytes 36872 | tf_op jit(solution)/shard_map/ppermute | solution.py:277
  89.7 4.4 %collective-permute-start.14 = (f32[2,8,192]{2,1,0:T(8,128)S(1)}, f32[2,8,192]{2,1,0:T(8,128)S(1)}, u32[]{:S(2)}, u32[]{:S(2)}) collective-permute-start(f32[2,8,192]{2,1,0:T(8,128)S(1)} %pad_maximum_fusion.1), channel_id=1, source_target_pairs={{0,1},{1,2},{2,3},{3,0},{4,5},{5,6},{6,7},{7,4},{8,9},{9,10},{10,1... | collective-permute-start | bytes 36872 | tf_op jit(solution)/shard_map/ppermute | solution.py:277
  91.6 3.1 %collective-permute-start.15 = (f32[2,8,192]{2,1,0:T(8,128)S(1)}, f32[2,8,192]{2,1,0:T(8,128)S(1)}, u32[]{:S(2)}, u32[]{:S(2)}) collective-permute-start(f32[2,8,192]{2,1,0:T(8,128)S(1)} %pad_maximum_fusion.1), channel_id=1, source_target_pairs={{0,3},{1,0},{2,1},{3,2},{4,7},{5,4},{6,5},{7,6},{8,11},{9,8},{10,9... | collective-permute-start | bytes 36872 | tf_op jit(solution)/shard_map/ppermute | solution.py:277

commit v4 on v3

--- a/solution.py
+++ b/solution.py
@@ -245,17 +245,20 @@
     writes = [
         pltpu.make_async_copy(held.at[r], out.at[r], out_sems.at[i]) for i, r in enumerate(rows)
     ]
-    for read in reads:
+    ahead = 2
+    for read in reads[:ahead]:
         read.start()
-    for read, write in zip(reads, writes):
+    for i, (read, write) in enumerate(zip(reads, writes)):
         read.wait()
+        if i + ahead < n_copies:
+            reads[i + ahead].start()
         write.start()
     for write in writes:
         write.wait()
 
 
 def store(got):
-    n_copies = 4
+    n_copies = 8
     return pl.pallas_call(
         store_kernel,
         out_shape=jax.ShapeDtypeStruct(got.shape, got.dtype),

time: 178 us -> 181 us (1.017)
  Pallas kernels: 19.6 us -> 22 us
    pallas_call x1, Pallas kernels: 5.16 us -> 7.6 us  [store(): pl.pallas_call(store_kernel, out_shape=jax.ShapeDtypeStruct(got.shape, go...]
where the time goes in v4:
time: 181 us; the launch traced here: 180 us
  waiting for transfers between devices  109 us (60%)
  starting transfers between devices  40 us (22%)
  Pallas kernels  22 us (12%)
  local copies, waits for them, and re-layouts  7.12 us (4%)
    all_to_all x1, waiting for transfers between devices, body(): lax.all_to_all(outgoing, 'post', split_axis=0, concat_axis=0, tiled=True)  76.8 us
    ppermute x7, waiting for transfers between devices, shift_in_plane(): return lax.ppermute(x, 'post', pairs)  16.7 us
    ppermute x9, starting transfers between devices, shift(): return lax.ppermute(x, axis, [(i, (i + k) % n) for i in range(n)])  16.3 us
    ppermute x9, waiting for transfers between devices, shift(): return lax.ppermute(x, axis, [(i, (i + k) % n) for i in range(n)])  9.62 us
    all_to_all x1, starting transfers between devices, body(): lax.all_to_all(copies, 'post', split_axis=0, concat_axis=0, tiled=True, a...  9.03 us
    all_to_all x1, starting transfers between devices, body(): lax.all_to_all(outgoing, 'post', split_axis=0, concat_axis=0, tiled=True)  7.66 us
    pallas_call x1, Pallas kernels, store(): pl.pallas_call(store_kernel, out_shape=jax.ShapeDtypeStruct(got.shape, go...  7.6 us
    ppermute x7, starting transfers between devices, shift_in_plane(): return lax.ppermute(x, 'post', pairs)  6.94 us
  transfers between devices with their start and end apart: 18, of which 11 were waited for; matrix products, arithmetic and copies ran while one was open for 4% of the time, Pallas kernels for 6%

profile of v4, /device:TPU:1, one launch (start us, length us, event | category | flops | bytes accessed | tf_op | source)
XLA Modules:
  0.0 180.0 jit_solution(8451023831677874149)
XLA Ops:
  0.6 3.6 %centroids.1 = (f32[64,256]{1,0:T(8,128)}, bf16[8,64,256]{2,1,0:T(8,128)(2,1)}) custom-call(s32[32]{0:T(128)} %lengths_hbm.3, s32[32,192]{1,0:T(8,128)} %labels_hbm.3, bf16[32,192,256]{2,1,0:T(8,128)(2,1)} %vectors_hbm.2), custom_call_target="tpu_custom_call" | custom-call | flops 100000000 | bytes 4194304 | tf_op jit(solution)/shard_map/centroids/pallas_call | solution.py:74
  4.3 9.0 %all-to-all-start = ((bf16[8,64,256]{2,1,0:T(8,128)(2,1)}), bf16[8,64,256]{2,1,0:T(8,128)(2,1)S(1)}, u32[]{:S(2)}, u32[]{:S(2)}) async-start(bf16[8,64,256]{2,1,0:T(8,128)(2,1)} %get-tuple-element.12), calls=%async_computation | async-start | bytes 524288 | tf_op jit(solution)/shard_map/all_to_all | solution.py:311
  13.3 4.9 %pack.1 = bf16[128,96,256]{2,1,0:T(8,128)(2,1)} custom-call(s32[2,32]{1,0:T(2,128)} %bitcast.51, s32[32]{0:T(128)} %lengths_hbm.3, s32[32,192]{1,0:T(8,128)} %labels_hbm.3, bf16[32,192,256]{2,1,0:T(8,128)(2,1)} %vectors_hbm.2), custom_call_target="tpu_custom_call" | custom-call | flops 1000000000 | bytes 16777216 | tf_op jit(solution)/shard_map/pack/pallas_call | solution.py:180
  18.2 5.5 %all-to-all-done = bf16[8,64,256]{2,1,0:T(8,128)(2,1)S(1)} async-done(((bf16[8,64,256]{2,1,0:T(8,128)(2,1)}), bf16[8,64,256]{2,1,0:T(8,128)(2,1)S(1)}, u32[]{:S(2)}, u32[]{:S(2)}) %all-to-all-start) | async-done | bytes 262176 | tf_op jit(solution)/shard_map/all_to_all | solution.py:311
  23.7 7.7 %all-to-all-start.1 = ((bf16[64,2,96,256]{3,2,1,0:T(8,128)(2,1)}), bf16[64,2,96,256]{3,2,1,0:T(8,128)(2,1)}, u32[]{:S(2)}, u32[]{:S(2)}) async-start(bf16[64,2,96,256]{3,2,1,0:T(8,128)(2,1)} %bitcast.42), calls=%async_computation.1 | async-start | bytes 12582912 | tf_op jit(solution)/shard_map/all_to_all | solution.py:321
  31.4 0.0 copy-start.6
  31.4 1.4 collective-permute-start.3
  32.8 2.6 %collective-permute-start.4 = (bf16[128,256]{1,0:T(8,128)(2,1)S(1)}, bf16[128,256]{1,0:T(8,128)(2,1)S(1)}, u32[]{:S(2)}, u32[]{:S(2)}) collective-permute-start(bf16[128,256]{1,0:T(8,128)(2,1)S(1)} %bitcast.46), channel_id=1, source_target_pairs={{0,2},{1,3},{2,0},{3,1},{4,6},{5,7},{6,4},{7,5},{8,10},{9,11},{10,... | collective-permute-start | bytes 196616 | tf_op jit(solution)/shard_map/ppermute | solution.py:280
  35.4 1.1 collective-permute-start.5
  36.5 0.0 collective-permute-done.3
  36.5 1.6 collective-permute-done.4
  38.1 0.9 collective-permute-done.5
  39.0 1.6 collective-permute-start.6
  40.5 1.5 collective-permute-start.7
  42.1 1.6 collective-permute-start.8
  43.6 0.2 collective-permute-start
  43.8 3.3 %collective-permute-start.1 = (bf16[8,192,256]{2,1,0:T(8,128)(2,1)S(1)}, bf16[8,192,256]{2,1,0:T(8,128)(2,1)S(1)}, u32[]{:S(2)}, u32[]{:S(2)}) collective-permute-start(bf16[8,192,256]{2,1,0:T(8,128)(2,1)S(1)} %copy-done), channel_id=1, source_target_pairs={{0,2},{1,3},{2,0},{3,1},{4,6},{5,7},{6,4},{7,5},{8,10},{9,11},{10,... | collective-permute-start | bytes 2359304 | tf_op jit(solution)/shard_map/ppermute | solution.py:280
  47.1 10.7 %collective-permute-done.6.refs_5_ = bf16[4,128,256]{2,1,0:T(8,128)(2,1)} collective-permute-done((bf16[4,128,256]{2,1,0:T(8,128)(2,1)S(1)}, bf16[4,128,256]{2,1,0:T(8,128)(2,1)}, u32[]{:S(2)}, u32[]{:S(2)}) %collective-permute-start.6) | collective-permute-done | bytes 262176 | tf_op jit(solution)/shard_map/ppermute | solution.py:289
  57.8 2.7 %collective-permute-start.2 = (bf16[8,192,256]{2,1,0:T(8,128)(2,1)S(1)}, bf16[8,192,256]{2,1,0:T(8,128)(2,1)S(1)}, u32[]{:S(2)}, u32[]{:S(2)}) collective-permute-start(bf16[8,192,256]{2,1,0:T(8,128)(2,1)S(1)} %copy-done), channel_id=1, source_target_pairs={{0,3},{1,0},{2,1},{3,2},{4,7},{5,4},{6,5},{7,6},{8,11},{9,8},{10,9... | collective-permute-start | bytes 2359304 | tf_op jit(solution)/shard_map/ppermute | solution.py:280
  60.6 1.0 collective-permute-start.9
  61.5 5.7 %collective-permute-done.8.refs_7_ = bf16[4,128,256]{2,1,0:T(8,128)(2,1)S(1)} collective-permute-done((bf16[4,128,256]{2,1,0:T(8,128)(2,1)S(1)}, bf16[4,128,256]{2,1,0:T(8,128)(2,1)S(1)}, u32[]{:S(2)}, u32[]{:S(2)}) %collective-permute-start.8) | collective-permute-done | bytes 262176 | tf_op jit(solution)/shard_map/ppermute | solution.py:289
  67.2 0.7 copy-done.3
  67.9 0.7 collective-permute-start.10
  68.7 2.5 %constant_dynamic-slice_fusion = (s32[32,64]{0,1:T(8,128)}, s32[32,64]{0,1:T(8,128)}, s32[32,64]{0,1:T(8,128)}, s32[32,64]{0,1:T(8,128)}, s32[32,64]{0,1:T(8,128...) fusion(s32[2048,64]{0,1:T(8,128)} %param.12, ...), kind=kLoop, calls=%fused_computation.18 | loop fusion | bytes 262208 | tf_op jit(solution)/shard_map/dynamic_slice | solution.py:346
  71.2 1.2 concatenate.3
  72.4 0.0 collective-permute-done.9.refs_8_
  72.4 0.1 collective-permute-start.11
  72.5 0.0 collective-permute-done.10.refs_9_
  72.5 0.5 collective-permute-start.12
  73.0 0.2 compare_reduce_fusion
  73.2 0.9 copy.12
  74.1 0.4 multiply_reduce_fusion
  74.5 0.2 collective-permute-done.12.refs_11_
  74.7 4.4 %collective-permute-done.1.refs_2_ = bf16[8,192,256]{2,1,0:T(8,128)(2,1)S(1)} collective-permute-done((bf16[8,192,256]{2,1,0:T(8,128)(2,1)S(1)}, bf16[8,192,256]{2,1,0:T(8,128)(2,1)S(1)}, u32[]{:S(2)}, u32[]{:S(2)}) %collective-permute-start.1) | collective-permute-done | bytes 786464 | tf_op jit(solution)/shard_map/ppermute | solution.py:280
  79.1 1.3 collective-permute-done.2.refs_3_
  80.4 1.1 broadcast_in_dim.5
  81.6 0.0 copy-start.5
  81.6 0.0 copy-start.7
  81.6 5.9 %score.1 = f32[8,192]{1,0:T(8,128)S(1)} custom-call(bf16[8,192,256]{2,1,0:T(8,128)(2,1)S(1)} %copy-done, bf16[8,192,256]{2,1,0:T(8,128)(2,1)S(1)} %collective-permute-done.refs_1_, bf16[8,192,256]{2,1,0:T(8,128)(2,1)S(1)} %collective-permute-done.1.refs_2_, bf16[8,192,256]{2,1,0:T(8,128)(2,1)S(1)} %collective-permute-done.2.refs_3_, ...), custom_call_target="tpu_custom_call" | custom-call | flops 4000000000 | bytes 6291456 | tf_op jit(solution)/shard_map/score/pallas_call | solution.py:227
  87.5 2.2 %collective-permute-start.13 = (f32[2,8,192]{2,1,0:T(8,128)S(1)}, f32[2,8,192]{2,1,0:T(8,128)S(1)}, u32[]{:S(2)}, u32[]{:S(2)}) collective-permute-start(f32[2,8,192]{2,1,0:T(8,128)S(1)} %pad_maximum_fusion.1), channel_id=1, source_target_pairs={{0,2},{1,3},{2,0},{3,1},{4,6},{5,7},{6,4},{7,5},{8,10},{9,11},{10,... | collective-permute-start | bytes 36872 | tf_op jit(solution)/shard_map/ppermute | solution.py:280
  89.7 1.9 %collective-permute-start.14 = (f32[2,8,192]{2,1,0:T(8,128)S(1)}, f32[2,8,192]{2,1,0:T(8,128)S(1)}, u32[]{:S(2)}, u32[]{:S(2)}) collective-permute-start(f32[2,8,192]{2,1,0:T(8,128)S(1)} %pad_maximum_fusion.1), channel_id=1, source_target_pairs={{0,1},{1,2},{2,3},{3,0},{4,5},{5,6},{6,7},{7,4},{8,9},{9,10},{10,1... | collective-permute-start | bytes 36872 | tf_op jit(solution)/shard_map/ppermute | solution.py:280
  91.6 1.0 collective-permute-start.15
  92.6 0.7 reshape.34
  93.3 0.8 collective-permute-done.14
  94.1 0.6 collective-permute-done.15
  94.7 0.7 fusion.4
  95.4 76.8 %all-to-all-done.1.got = bf16[64,2,96,256]{3,2,1,0:T(8,128)(2,1)} async-done(((bf16[64,2,96,256]{3,2,1,0:T(8,128)(2,1)}), bf16[64,2,96,256]{3,2,1,0:T(8,128)(2,1)}, u32[]{:S(2)}, u32[]{:S(2)}) %all-to-all-start.1) | async-done | bytes 6291488 | tf_op jit(solution)/shard_map/all_to_all | solution.py:321
  172.3 7.6 %store.1 = bf16[64,2,96,256]{3,2,1,0:T(8,128)(2,1)} custom-call(bf16[64,2,96,256]{3,2,1,0:T(8,128)(2,1)} %all-to-all-done.1.got), custom_call_target="tpu_custom_call" | custom-call | bytes 12582912 | tf_op jit(solution)/shard_map/store/pallas_call | solution.py:262
  (22 shorter events, 0.1 us)
Async XLA Ops:
  4.3 19.4 %all-to-all-start = ((bf16[8,64,256]{2,1,0:T(8,128)(2,1)}), bf16[8,64,256]{2,1,0:T(8,128)(2,1)S(1)}, u32[]{:S(2)}, u32[]{:S(2)}) async-start(bf16[8,64,256]{2,1,0:T(8,128)(2,1)} %get-tuple-element.12), calls=%async_computation | async-start | bytes 524288 | tf_op jit(solution)/shard_map/all_to_all | solution.py:311
  23.7 19.9 %copy-start = (bf16[8,192,256]{2,1,0:T(8,128)(2,1)S(1)}, bf16[8,192,256]{2,1,0:T(8,128)(2,1)}, u32[]{:S(2)}) copy-start(bf16[8,192,256]{2,1,0:T(8,128)(2,1)} %refs_0_) | copy-start | bytes 2359300
  23.7 148.6 %all-to-all-start.1 = ((bf16[64,2,96,256]{3,2,1,0:T(8,128)(2,1)}), bf16[64,2,96,256]{3,2,1,0:T(8,128)(2,1)}, u32[]{:S(2)}, u32[]{:S(2)}) async-start(bf16[64,2,96,256]{3,2,1,0:T(8,128)(2,1)} %bitcast.42), calls=%async_computation.1 | async-start | bytes 12582912 | tf_op jit(solution)/shard_map/all_to_all | solution.py:321
  31.4 42.7 %copy-start.6 = (bf16[8,256]{1,0:T(8,128)(2,1)S(1)}, bf16[8,256]{1,0:T(8,128)(2,1)}, u32[]{:S(2)}) copy-start(bf16[8,256]{1,0:T(8,128)(2,1)} %param.14) | copy-start | bytes 12292
  31.4 5.1 %collective-permute-start.3 = (bf16[128,256]{1,0:T(8,128)(2,1)S(1)}, bf16[128,256]{1,0:T(8,128)(2,1)S(1)}, u32[]{:S(2)}, u32[]{:S(2)}) collective-permute-start(bf16[128,256]{1,0:T(8,128)(2,1)S(1)} %bitcast.48), channel_id=1, source_target_pairs={{0,1},{1,2},{2,3},{3,0},{4,5},{5,6},{6,7},{7,4},{8,9},{9,10},{10,1... | collective-permute-start | bytes 196616 | tf_op jit(solution)/shard_map/ppermute | solution.py:280
  32.8 5.3 %collective-permute-start.4 = (bf16[128,256]{1,0:T(8,128)(2,1)S(1)}, bf16[128,256]{1,0:T(8,128)(2,1)S(1)}, u32[]{:S(2)}, u32[]{:S(2)}) collective-permute-start(bf16[128,256]{1,0:T(8,128)(2,1)S(1)} %bitcast.46), channel_id=1, source_target_pairs={{0,2},{1,3},{2,0},{3,1},{4,6},{5,7},{6,4},{7,5},{8,10},{9,11},{10,... | collective-permute-start | bytes 196616 | tf_op jit(solution)/shard_map/ppermute | solution.py:280
  35.4 3.5 %collective-permute-start.5 = (bf16[128,256]{1,0:T(8,128)(2,1)S(1)}, bf16[128,256]{1,0:T(8,128)(2,1)S(1)}, u32[]{:S(2)}, u32[]{:S(2)}) collective-permute-start(bf16[128,256]{1,0:T(8,128)(2,1)S(1)} %bitcast.45), channel_id=1, source_target_pairs={{0,3},{1,0},{2,1},{3,2},{4,7},{5,4},{6,5},{7,6},{8,11},{9,8},{10,9... | collective-permute-start | bytes 196616 | tf_op jit(solution)/shard_map/ppermute | solution.py:280
  39.0 18.8 %collective-permute-start.6 = (bf16[4,128,256]{2,1,0:T(8,128)(2,1)S(1)}, bf16[4,128,256]{2,1,0:T(8,128)(2,1)}, u32[]{:S(2)}, u32[]{:S(2)}) collective-permute-start(bf16[4,128,256]{2,1,0:T(8,128)(2,1)S(1)} %pad_maximum_fusion.refs_4_), channel_id=1, source_target_pairs={{0,64},{4,68},{8,72},{12,76},{16,80},{20,84},{24,88},{28,92},{32,9... | collective-permute-start | bytes 786440 | tf_op jit(solution)/shard_map/ppermute | solution.py:289
  40.5 20.0 %collective-permute-start.7 = (bf16[4,128,256]{2,1,0:T(8,128)(2,1)S(1)}, bf16[4,128,256]{2,1,0:T(8,128)(2,1)S(1)}, u32[]{:S(2)}, u32[]{:S(2)}) collective-permute-start(bf16[4,128,256]{2,1,0:T(8,128)(2,1)S(1)} %pad_maximum_fusion.refs_4_), channel_id=1, source_target_pairs={{0,192},{4,196},{8,200},{12,204},{16,208},{20,212},{24,216},{28,22... | collective-permute-start | bytes 786440 | tf_op jit(solution)/shard_map/ppermute | solution.py:289
  42.1 25.2 %collective-permute-start.8 = (bf16[4,128,256]{2,1,0:T(8,128)(2,1)S(1)}, bf16[4,128,256]{2,1,0:T(8,128)(2,1)S(1)}, u32[]{:S(2)}, u32[]{:S(2)}) collective-permute-start(bf16[4,128,256]{2,1,0:T(8,128)(2,1)S(1)} %pad_maximum_fusion.refs_4_), channel_id=1, source_target_pairs={{0,128},{4,132},{8,136},{12,140},{16,144},{20,148},{24,152},{28,15... | collective-permute-start | bytes 786440 | tf_op jit(solution)/shard_map/ppermute | solution.py:289
  43.6 31.1 %collective-permute-start = (bf16[8,192,256]{2,1,0:T(8,128)(2,1)S(1)}, bf16[8,192,256]{2,1,0:T(8,128)(2,1)S(1)}, u32[]{:S(2)}, u32[]{:S(2)}) collective-permute-start(bf16[8,192,256]{2,1,0:T(8,128)(2,1)S(1)} %copy-done), channel_id=1, source_target_pairs={{0,1},{1,2},{2,3},{3,0},{4,5},{5,6},{6,7},{7,4},{8,9},{9,10},{10,1... | collective-permute-start | bytes 2359304 | tf_op jit(solution)/shard_map/ppermute | solution.py:280
  43.8 35.3 %collective-permute-start.1 = (bf16[8,192,256]{2,1,0:T(8,128)(2,1)S(1)}, bf16[8,192,256]{2,1,0:T(8,128)(2,1)S(1)}, u32[]{:S(2)}, u32[]{:S(2)}) collective-permute-start(bf16[8,192,256]{2,1,0:T(8,128)(2,1)S(1)} %copy-done), channel_id=1, source_target_pairs={{0,2},{1,3},{2,0},{3,1},{4,6},{5,7},{6,4},{7,5},{8,10},{9,11},{10,... | collective-permute-start | bytes 2359304 | tf_op jit(solution)/shard_map/ppermute | solution.py:280
  57.8 22.6 %collective-permute-start.2 = (bf16[8,192,256]{2,1,0:T(8,128)(2,1)S(1)}, bf16[8,192,256]{2,1,0:T(8,128)(2,1)S(1)}, u32[]{:S(2)}, u32[]{:S(2)}) collective-permute-start(bf16[8,192,256]{2,1,0:T(8,128)(2,1)S(1)} %copy-done), channel_id=1, source_target_pairs={{0,3},{1,0},{2,1},{3,2},{4,7},{5,4},{6,5},{7,6},{8,11},{9,8},{10,9... | collective-permute-start | bytes 2359304 | tf_op jit(solution)/shard_map/ppermute | solution.py:280
  60.6 6.7 %copy-start.1 = (bf16[4,128,256]{2,1,0:T(8,128)(2,1)}, bf16[4,128,256]{2,1,0:T(8,128)(2,1)S(1)}, u32[]{:S(2)}) copy-start(bf16[4,128,256]{2,1,0:T(8,128)(2,1)S(1)} %collective-permute-done.7.refs_6_) | copy-start | bytes 786436
  60.6 11.8 %collective-permute-start.9 = (bf16[4,128,256]{2,1,0:T(8,128)(2,1)S(1)}, bf16[4,128,256]{2,1,0:T(8,128)(2,1)}, u32[]{:S(2)}, u32[]{:S(2)}) collective-permute-start(bf16[4,128,256]{2,1,0:T(8,128)(2,1)S(1)} %pad_maximum_fusion.refs_4_), channel_id=1, source_target_pairs={{0,4},{4,0},{8,12},{12,8},{16,20},{20,16},{24,28},{28,24},{32,36},... | collective-permute-start | bytes 786440 | tf_op jit(solution)/shard_map/ppermute | solution.py:289
  67.2 0.7 copy-start.3
  67.9 4.6 %collective-permute-start.10 = (bf16[4,128,256]{2,1,0:T(8,128)(2,1)}, bf16[4,128,256]{2,1,0:T(8,128)(2,1)}, u32[]{:S(2)}, u32[]{:S(2)}) collective-permute-start(bf16[4,128,256]{2,1,0:T(8,128)(2,1)} %collective-permute-done.6.refs_5_), channel_id=1, source_target_pairs={{0,4},{4,0},{8,12},{12,8},{16,20},{20,16},{24,28},{28,24},{32,36},... | collective-permute-start | bytes 786440 | tf_op jit(solution)/shard_map/ppermute | solution.py:289
  72.4 2.1 %collective-permute-start.11 = (bf16[4,128,256]{2,1,0:T(8,128)(2,1)}, bf16[4,128,256]{2,1,0:T(8,128)(2,1)}, u32[]{:S(2)}, u32[]{:S(2)}) collective-permute-start(bf16[4,128,256]{2,1,0:T(8,128)(2,1)} %copy-done.1), channel_id=1, source_target_pairs={{0,4},{4,0},{8,12},{12,8},{16,20},{20,16},{24,28},{28,24},{32,36},... | collective-permute-start | bytes 786440 | tf_op jit(solution)/shard_map/ppermute | solution.py:289
  72.5 2.2 %collective-permute-start.12 = (bf16[4,128,256]{2,1,0:T(8,128)(2,1)}, bf16[4,128,256]{2,1,0:T(8,128)(2,1)}, u32[]{:S(2)}, u32[]{:S(2)}) collective-permute-start(bf16[4,128,256]{2,1,0:T(8,128)(2,1)} %copy-done.3), channel_id=1, source_target_pairs={{0,4},{4,0},{8,12},{12,8},{16,20},{20,16},{24,28},{28,24},{32,36},... | collective-permute-start | bytes 786440 | tf_op jit(solution)/shard_map/ppermute | solution.py:289
  74.1 7.5 %copy-start.2 = (bf16[4,128,256]{2,1,0:T(8,128)(2,1)S(1)}, bf16[4,128,256]{2,1,0:T(8,128)(2,1)}, u32[]{:S(2)}) copy-start(bf16[4,128,256]{2,1,0:T(8,128)(2,1)} %copy-done.1) | copy-start | bytes 786436
  74.1 7.5 %copy-start.4 = (bf16[4,128,256]{2,1,0:T(8,128)(2,1)S(1)}, bf16[4,128,256]{2,1,0:T(8,128)(2,1)}, u32[]{:S(2)}) copy-start(bf16[4,128,256]{2,1,0:T(8,128)(2,1)} %copy-done.3) | copy-start | bytes 786436
  81.6 11.0 %copy-start.5 = (f32[64,256]{1,0:T(8,128)S(1)}, f32[64,256]{1,0:T(8,128)}, u32[]{:S(2)}) copy-start(f32[64,256]{1,0:T(8,128)} %get-tuple-element.16) | copy-start | bytes 196612
  81.6 13.1 %copy-start.7 = (s32[8]{0:T(128)S(1)}, s32[8]{0:T(128)}, u32[]{:S(2)}) copy-start(s32[8]{0:T(128)} %param.15) | copy-start | bytes 100
  87.5 5.7 %collective-permute-start.13 = (f32[2,8,192]{2,1,0:T(8,128)S(1)}, f32[2,8,192]{2,1,0:T(8,128)S(1)}, u32[]{:S(2)}, u32[]{:S(2)}) collective-permute-start(f32[2,8,192]{2,1,0:T(8,128)S(1)} %pad_maximum_fusion.1), channel_id=1, source_target_pairs={{0,2},{1,3},{2,0},{3,1},{4,6},{5,7},{6,4},{7,5},{8,10},{9,11},{10,... | collective-permute-start | bytes 36872 | tf_op jit(solution)/shard_map/ppermute | solution.py:280
  89.7 4.4 %collective-permute-start.14 = (f32[2,8,192]{2,1,0:T(8,128)S(1)}, f32[2,8,192]{2,1,0:T(8,128)S(1)}, u32[]{:S(2)}, u32[]{:S(2)}) collective-permute-start(f32[2,8,192]{2,1,0:T(8,128)S(1)} %pad_maximum_fusion.1), channel_id=1, source_target_pairs={{0,1},{1,2},{2,3},{3,0},{4,5},{5,6},{6,7},{7,4},{8,9},{9,10},{10,1... | collective-permute-start | bytes 36872 | tf_op jit(solution)/shard_map/ppermute | solution.py:280
  91.6 3.1 %collective-permute-start.15 = (f32[2,8,192]{2,1,0:T(8,128)S(1)}, f32[2,8,192]{2,1,0:T(8,128)S(1)}, u32[]{:S(2)}, u32[]{:S(2)}) collective-permute-start(f32[2,8,192]{2,1,0:T(8,128)S(1)} %pad_maximum_fusion.1), channel_id=1, source_target_pairs={{0,3},{1,0},{2,1},{3,2},{4,7},{5,4},{6,5},{7,6},{8,11},{9,8},{10,9... | collective-permute-start | bytes 36872 | tf_op jit(solution)/shard_map/ppermute | solution.py:280
